TPU v7x, 128 devices: a whole 4x4x4 slice. The times are simulated.
128 devices in a mesh: row: 8 (over x_hi, z), col: 16 (over x_lo, y, core).
Axes of the slice: x: 4 (x_hi: 2, x_lo: 2; x = x_hi * 2 + x_lo), y: 4, z: 4, core: 2. Of those that a mesh axis runs over, the one named last changes fastest.
Arguments:
- latent: float32 [2, 2048, 4096], P(None, 'row', 'col'), may hold values from -3 to 3
- momentum: float32 [2, 2048, 4096], P(None, 'row', 'col'), may hold values from -4 to 4
- hyper_params: float32 [2, 2], replicated, may hold values from 0.3 to 0.7
- velocity: float32 [2, 2], replicated, may hold values from -3 to 3
- step_size: float32 [2], replicated, may hold values from 0.08 to 0.12
- counts: int32 [2048, 4096], P('row', 'col'), may hold values from 0 to 7
- kappa_field: float32 [2048, 4096], P('row', 'col'), may hold values from 0.1 to 1
Outputs:
- latent_out: float32 [2, 2048, 4096], P(None, 'row', 'col')
- momentum_out: float32 [2, 2048, 4096], P(None, 'row', 'col')
- hyper_out: float32 [2, 2], replicated
- velocity_out: float32 [2, 2], replicated
All inputs are finite; a program needn't handle non-finite values.
Results may differ from a plain program's by a relative error of at most 0.0001.
Values sent between devices are 32-bit elements; how exact they have to be, the bound alone decides.
No kernel may reach another device: no remote copies, remote signals or barrier semaphores. Data moves between devices by JAX's collectives and lax.ppermute only.
A program may use at most 64 MiB of HBM per device.

v0:
```python
import jax
import jax.numpy as jnp
from jax import lax
from jax.sharding import Mesh
from jax.sharding import PartitionSpec as P

STEPS = 10
ROW_COL = ("row_0", "row_1", "col_0", "col_1", "col_2")
ROW = ("row_0", "row_1")
COL = ("col_0", "col_1", "col_2")


def over_axes(x, axes):
    for axis in axes:
        x = lax.psum(x, axis)
    return x


def padded(cells, sides, width):
    for axis, dim in sides:
        count = lax.axis_size(axis)
        head = lax.slice_in_dim(cells, 0, width, axis=dim)
        tail = lax.slice_in_dim(cells, cells.shape[dim] - width, cells.shape[dim], axis=dim)
        cells = jnp.concatenate(
            [
                lax.ppermute(tail, axis, [(i, (i + 1) % count) for i in range(count)]),
                cells,
                lax.ppermute(head, axis, [((i + 1) % count, i) for i in range(count)]),
            ],
            axis=dim,
        )
    return cells


def local_gradient(widened, count_part, kappa_part, offset, tau_value, margin):
    center = widened[:, 1:-1, 1:-1]
    beside = (
        widened[:, :-2, 1:-1] + widened[:, 2:, 1:-1] + widened[:, 1:-1, :-2] + widened[:, 1:-1, 2:]
    )
    applied = (kappa_part + 4.0) * center - beside
    intensity = jnp.exp(offset[:, None, None] + center)
    gradient = tau_value[:, None, None] * applied - count_part + intensity
    weighted = center * applied
    excess_terms = intensity - count_part
    if margin:
        weighted = weighted[:, margin:-margin, margin:-margin]
        excess_terms = excess_terms[:, margin:-margin, margin:-margin]
    return (gradient, jnp.sum(weighted, axis=(1, 2)), jnp.sum(excess_terms, axis=(1, 2)))


def acceleration(quadratic, excess, tau_value, total):
    stacked = jnp.stack([quadratic, excess])
    summed = over_axes(stacked, ROW_COL)
    return jnp.stack([summed[1] / total, 0.5 * tau_value * summed[0] / total - 0.5])


def trimmed(array, layers):
    return array[..., layers:-layers, layers:-layers]


def shards(latent, momentum, hyper_params, velocity, step_size, counts, kappa_field):
    count_float = counts.astype(jnp.float32)
    total = float(latent.shape[1] * latent.shape[2] * lax.axis_size(ROW) * lax.axis_size(COL))
    size_grid = step_size[:, None, None]
    layers_deep = 5
    wide_counts, wide_kappa = (
        padded(count_float, ((ROW, 0), (COL, 1)), layers_deep),
        padded(kappa_field, ((ROW, 0), (COL, 1)), layers_deep),
    )
    field, moment, params, speed = (latent, momentum, hyper_params, velocity)
    accel = jnp.zeros_like(velocity)
    for index_block in range(STEPS // layers_deep):
        field, moment = (
            padded(field, ((ROW, 1), (COL, 2)), layers_deep + 1),
            padded(moment, ((ROW, 1), (COL, 2)), layers_deep + 1),
        )
        moment = trimmed(moment, 1)
        tau_value = jnp.exp(params[1])
        gradient, quadratic, excess = local_gradient(
            field, wide_counts, wide_kappa, params[0], tau_value, layers_deep
        )
        if index_block == 0:
            accel = acceleration(quadratic, excess, tau_value, total)
        for inner in range(layers_deep):
            width_now = layers_deep - inner
            field = trimmed(field, 1)
            moment = moment - 0.5 * size_grid * gradient
            speed = speed - 0.5 * step_size * accel
            field = field + size_grid * moment
            params = params + step_size * speed
            tau_value = jnp.exp(params[1])
            gradient, quadratic, excess = local_gradient(
                field,
                trimmed(wide_counts, inner + 1),
                trimmed(wide_kappa, inner + 1),
                params[0],
                tau_value,
                width_now - 1,
            )
            accel = acceleration(quadratic, excess, tau_value, total)
            moment = trimmed(moment, 1) - 0.5 * size_grid * gradient
            speed = speed - 0.5 * step_size * accel
        field = trimmed(field, 1)
    return (field, moment, params, speed)


def solution(mesh):
    torus = Mesh(mesh.devices.reshape(2, 4, 2, 4, 2), ("row_0", "row_1", "col_0", "col_1", "col_2"))
    return jax.shard_map(
        shards,
        mesh=torus,
        in_specs=(P(None, ROW, COL), P(None, ROW, COL), P(), P(), P(), P(ROW, COL), P(ROW, COL)),
        out_specs=(P(None, ROW, COL), P(None, ROW, COL), P(), P()),
        check_vma=False,
    )
```

profile of v0, /device:TPU:1, one launch (start us, length us, event | category | flops | bytes accessed | tf_op | source)
XLA Modules:
  0.0 473.3 jit_solution(1764007279754260774)
XLA Ops:
  1.4 7.0 %collective-permute-start.1 = (f32[2,6,256]{2,1,0:T(8,128)S(1)}, f32[2,6,256]{2,1,0:T(8,128)S(1)}, u32[]{:S(2)}, u32[]{:S(2)}) collective-permute-start(f32[2,6,256]{2,1,0:T(8,128)S(1)} %get-tuple-element.87), channel_id=1, source_target_pairs={{16,0},{32,16},{48,32},{64,48},{80,64},{96,80},{112,96},{0,112},{1... | collective-permute-start | bytes 36872 | tf_op jit(solution)/shard_map/ppermute | solution.py:28
  55.6 6.7 %psum.386 = f32[2,2]{1,0:T(2,128)S(1)} all-reduce(f32[2,2]{1,0:T(2,128)S(1)} %psum.385), channel_id=1, replica_groups=mesh['row_0'=2,'row_1'=4,'col_0'=2,'col_1'=4,'col_2'=2] {'row_1'}, use_global_device_ids=true, to_apply=%region_3.0 | all-reduce | flops 4 | bytes 32 | tf_op jit(solution)/shard_map/psum | solution.py:15
  67.0 12.3 %psum.388 = f32[2,2]{1,0:T(2,128)S(1)} all-reduce(f32[2,2]{1,0:T(2,128)S(1)} %psum.387), channel_id=1, replica_groups=mesh['row_0'=2,'row_1'=4,'col_0'=2,'col_1'=4,'col_2'=2] {'col_1'}, use_global_device_ids=true, to_apply=%region_5.0 | all-reduce | flops 4 | bytes 32 | tf_op jit(solution)/shard_map/psum | solution.py:15
  80.3 9.2 %psum.389 = f32[2,2]{1,0:T(2,128)S(1)} all-reduce(f32[2,2]{1,0:T(2,128)S(1)} %psum.388), channel_id=1, replica_groups=mesh['row_0'=2,'row_1'=4,'col_0'=2,'col_1'=4,'col_2'=2] {'col_2'}, use_global_device_ids=true, to_apply=%region_6.0 | all-reduce | flops 4 | bytes 32 | tf_op jit(solution)/shard_map/psum | solution.py:15
  99.7 6.0 %psum.391 = f32[2,2]{1,0:T(2,128)S(1)} all-reduce(f32[2,2]{1,0:T(2,128)S(1)} %psum.390), channel_id=1, replica_groups=mesh['row_0'=2,'row_1'=4,'col_0'=2,'col_1'=4,'col_2'=2] {'row_1'}, use_global_device_ids=true, to_apply=%region_10.0 | all-reduce | flops 4 | bytes 32 | tf_op jit(solution)/shard_map/psum | solution.py:15
  110.4 7.7 %psum.393 = f32[2,2]{1,0:T(2,128)S(1)} all-reduce(f32[2,2]{1,0:T(2,128)S(1)} %psum.392), channel_id=1, replica_groups=mesh['row_0'=2,'row_1'=4,'col_0'=2,'col_1'=4,'col_2'=2] {'col_1'}, use_global_device_ids=true, to_apply=%region_12.0 | all-reduce | flops 4 | bytes 32 | tf_op jit(solution)/shard_map/psum | solution.py:15
  119.1 8.5 %psum.394 = f32[2,2]{1,0:T(2,128)S(1)} all-reduce(f32[2,2]{1,0:T(2,128)S(1)} %psum.393), channel_id=1, replica_groups=mesh['row_0'=2,'row_1'=4,'col_0'=2,'col_1'=4,'col_2'=2] {'col_2'}, use_global_device_ids=true, to_apply=%region_13.0 | all-reduce | flops 4 | bytes 32 | tf_op jit(solution)/shard_map/psum | solution.py:15
  137.1 7.7 %psum.396 = f32[2,2]{1,0:T(2,128)S(1)} all-reduce(f32[2,2]{1,0:T(2,128)S(1)} %psum.395), channel_id=1, replica_groups=mesh['row_0'=2,'row_1'=4,'col_0'=2,'col_1'=4,'col_2'=2] {'row_1'}, use_global_device_ids=true, to_apply=%region_17.0 | all-reduce | flops 4 | bytes 32 | tf_op jit(solution)/shard_map/psum | solution.py:15
  156.4 8.5 %psum.399 = f32[2,2]{1,0:T(2,128)S(1)} all-reduce(f32[2,2]{1,0:T(2,128)S(1)} %psum.398), channel_id=1, replica_groups=mesh['row_0'=2,'row_1'=4,'col_0'=2,'col_1'=4,'col_2'=2] {'col_2'}, use_global_device_ids=true, to_apply=%region_20.0 | all-reduce | flops 4 | bytes 32 | tf_op jit(solution)/shard_map/psum | solution.py:15
  174.4 6.0 %psum.401 = f32[2,2]{1,0:T(2,128)S(1)} all-reduce(f32[2,2]{1,0:T(2,128)S(1)} %psum.400), channel_id=1, replica_groups=mesh['row_0'=2,'row_1'=4,'col_0'=2,'col_1'=4,'col_2'=2] {'row_1'}, use_global_device_ids=true, to_apply=%region_24.0 | all-reduce | flops 4 | bytes 32 | tf_op jit(solution)/shard_map/psum | solution.py:15
  185.1 7.7 %psum.403 = f32[2,2]{1,0:T(2,128)S(1)} all-reduce(f32[2,2]{1,0:T(2,128)S(1)} %psum.402), channel_id=1, replica_groups=mesh['row_0'=2,'row_1'=4,'col_0'=2,'col_1'=4,'col_2'=2] {'col_1'}, use_global_device_ids=true, to_apply=%region_26.0 | all-reduce | flops 4 | bytes 32 | tf_op jit(solution)/shard_map/psum | solution.py:15
  193.7 8.5 %psum.404 = f32[2,2]{1,0:T(2,128)S(1)} all-reduce(f32[2,2]{1,0:T(2,128)S(1)} %psum.403), channel_id=1, replica_groups=mesh['row_0'=2,'row_1'=4,'col_0'=2,'col_1'=4,'col_2'=2] {'col_2'}, use_global_device_ids=true, to_apply=%region_27.0 | all-reduce | flops 4 | bytes 32 | tf_op jit(solution)/shard_map/psum | solution.py:15
  211.6 7.7 %psum.406 = f32[2,2]{1,0:T(2,128)S(1)} all-reduce(f32[2,2]{1,0:T(2,128)S(1)} %psum.405), channel_id=1, replica_groups=mesh['row_0'=2,'row_1'=4,'col_0'=2,'col_1'=4,'col_2'=2] {'row_1'}, use_global_device_ids=true, to_apply=%region_31.0 | all-reduce | flops 4 | bytes 32 | tf_op jit(solution)/shard_map/psum | solution.py:15
  229.1 8.5 %psum.409 = f32[2,2]{1,0:T(2,128)S(1)} all-reduce(f32[2,2]{1,0:T(2,128)S(1)} %psum.408), channel_id=1, replica_groups=mesh['row_0'=2,'row_1'=4,'col_0'=2,'col_1'=4,'col_2'=2] {'col_2'}, use_global_device_ids=true, to_apply=%region_34.0 | all-reduce | flops 4 | bytes 32 | tf_op jit(solution)/shard_map/psum | solution.py:15
  244.4 6.0 %psum.411 = f32[2,2]{1,0:T(2,128)S(1)} all-reduce(f32[2,2]{1,0:T(2,128)S(1)} %psum.410), channel_id=1, replica_groups=mesh['row_0'=2,'row_1'=4,'col_0'=2,'col_1'=4,'col_2'=2] {'row_1'}, use_global_device_ids=true, to_apply=%region_38.0 | all-reduce | flops 4 | bytes 32 | tf_op jit(solution)/shard_map/psum | solution.py:15
  254.1 7.7 %psum.413 = f32[2,2]{1,0:T(2,128)S(1)} all-reduce(f32[2,2]{1,0:T(2,128)S(1)} %psum.412), channel_id=1, replica_groups=mesh['row_0'=2,'row_1'=4,'col_0'=2,'col_1'=4,'col_2'=2] {'col_1'}, use_global_device_ids=true, to_apply=%region_40.0 | all-reduce | flops 4 | bytes 32 | tf_op jit(solution)/shard_map/psum | solution.py:15
  261.9 8.5 %psum.414 = f32[2,2]{1,0:T(2,128)S(1)} all-reduce(f32[2,2]{1,0:T(2,128)S(1)} %psum.413), channel_id=1, replica_groups=mesh['row_0'=2,'row_1'=4,'col_0'=2,'col_1'=4,'col_2'=2] {'col_2'}, use_global_device_ids=true, to_apply=%region_41.0 | all-reduce | flops 4 | bytes 32 | tf_op jit(solution)/shard_map/psum | solution.py:15
  303.6 6.0 %psum.416 = f32[2,2]{1,0:T(2,128)S(1)} all-reduce(f32[2,2]{1,0:T(2,128)S(1)} %psum.415), channel_id=1, replica_groups=mesh['row_0'=2,'row_1'=4,'col_0'=2,'col_1'=4,'col_2'=2] {'row_1'}, use_global_device_ids=true, to_apply=%region_45.0 | all-reduce | flops 4 | bytes 32 | tf_op jit(solution)/shard_map/psum | solution.py:15
  313.6 9.4 %psum.418 = f32[2,2]{1,0:T(2,128)S(1)} all-reduce(f32[2,2]{1,0:T(2,128)S(1)} %psum.417), channel_id=1, replica_groups=mesh['row_0'=2,'row_1'=4,'col_0'=2,'col_1'=4,'col_2'=2] {'col_1'}, use_global_device_ids=true, to_apply=%region_47.0 | all-reduce | flops 4 | bytes 32 | tf_op jit(solution)/shard_map/psum | solution.py:15
  323.0 8.7 %psum.419 = f32[2,2]{1,0:T(2,128)S(1)} all-reduce(f32[2,2]{1,0:T(2,128)S(1)} %psum.418), channel_id=1, replica_groups=mesh['row_0'=2,'row_1'=4,'col_0'=2,'col_1'=4,'col_2'=2] {'col_2'}, use_global_device_ids=true, to_apply=%region_48.0 | all-reduce | flops 4 | bytes 32 | tf_op jit(solution)/shard_map/psum | solution.py:15
  341.0 7.5 %psum.421 = f32[2,2]{1,0:T(2,128)S(1)} all-reduce(f32[2,2]{1,0:T(2,128)S(1)} %psum.420), channel_id=1, replica_groups=mesh['row_0'=2,'row_1'=4,'col_0'=2,'col_1'=4,'col_2'=2] {'row_1'}, use_global_device_ids=true, to_apply=%region_52.0 | all-reduce | flops 4 | bytes 32 | tf_op jit(solution)/shard_map/psum | solution.py:15
  352.3 7.7 %psum.423 = f32[2,2]{1,0:T(2,128)S(1)} all-reduce(f32[2,2]{1,0:T(2,128)S(1)} %psum.422), channel_id=1, replica_groups=mesh['row_0'=2,'row_1'=4,'col_0'=2,'col_1'=4,'col_2'=2] {'col_1'}, use_global_device_ids=true, to_apply=%region_54.0 | all-reduce | flops 4 | bytes 32 | tf_op jit(solution)/shard_map/psum | solution.py:15
  360.0 8.8 %psum.424 = f32[2,2]{1,0:T(2,128)S(1)} all-reduce(f32[2,2]{1,0:T(2,128)S(1)} %psum.423), channel_id=1, replica_groups=mesh['row_0'=2,'row_1'=4,'col_0'=2,'col_1'=4,'col_2'=2] {'col_2'}, use_global_device_ids=true, to_apply=%region_55.0 | all-reduce | flops 4 | bytes 32 | tf_op jit(solution)/shard_map/psum | solution.py:15
  378.1 6.0 %psum.426 = f32[2,2]{1,0:T(2,128)S(1)} all-reduce(f32[2,2]{1,0:T(2,128)S(1)} %psum.425), channel_id=1, replica_groups=mesh['row_0'=2,'row_1'=4,'col_0'=2,'col_1'=4,'col_2'=2] {'row_1'}, use_global_device_ids=true, to_apply=%region_59.0 | all-reduce | flops 4 | bytes 32 | tf_op jit(solution)/shard_map/psum | solution.py:15
  387.9 6.0 %psum.428 = f32[2,2]{1,0:T(2,128)S(1)} all-reduce(f32[2,2]{1,0:T(2,128)S(1)} %psum.427), channel_id=1, replica_groups=mesh['row_0'=2,'row_1'=4,'col_0'=2,'col_1'=4,'col_2'=2] {'col_1'}, use_global_device_ids=true, to_apply=%region_61.0 | all-reduce | flops 4 | bytes 32 | tf_op jit(solution)/shard_map/psum | solution.py:15
  393.8 8.6 %psum.429 = f32[2,2]{1,0:T(2,128)S(1)} all-reduce(f32[2,2]{1,0:T(2,128)S(1)} %psum.428), channel_id=1, replica_groups=mesh['row_0'=2,'row_1'=4,'col_0'=2,'col_1'=4,'col_2'=2] {'col_2'}, use_global_device_ids=true, to_apply=%region_62.0 | all-reduce | flops 4 | bytes 32 | tf_op jit(solution)/shard_map/psum | solution.py:15
  411.8 7.5 %psum.431 = f32[2,2]{1,0:T(2,128)S(1)} all-reduce(f32[2,2]{1,0:T(2,128)S(1)} %psum.430), channel_id=1, replica_groups=mesh['row_0'=2,'row_1'=4,'col_0'=2,'col_1'=4,'col_2'=2] {'row_1'}, use_global_device_ids=true, to_apply=%region_66.0 | all-reduce | flops 4 | bytes 32 | tf_op jit(solution)/shard_map/psum | solution.py:15
  423.1 7.7 %psum.433 = f32[2,2]{1,0:T(2,128)S(1)} all-reduce(f32[2,2]{1,0:T(2,128)S(1)} %psum.432), channel_id=1, replica_groups=mesh['row_0'=2,'row_1'=4,'col_0'=2,'col_1'=4,'col_2'=2] {'col_1'}, use_global_device_ids=true, to_apply=%region_68.0 | all-reduce | flops 4 | bytes 32 | tf_op jit(solution)/shard_map/psum | solution.py:15
  430.7 8.8 %psum.434 = f32[2,2]{1,0:T(2,128)S(1)} all-reduce(f32[2,2]{1,0:T(2,128)S(1)} %psum.433), channel_id=1, replica_groups=mesh['row_0'=2,'row_1'=4,'col_0'=2,'col_1'=4,'col_2'=2] {'col_2'}, use_global_device_ids=true, to_apply=%region_69.0 | all-reduce | flops 4 | bytes 32 | tf_op jit(solution)/shard_map/psum | solution.py:15
  446.3 6.0 %psum.436 = f32[2,2]{1,0:T(2,128)S(1)} all-reduce(f32[2,2]{1,0:T(2,128)S(1)} %psum.435), channel_id=1, replica_groups=mesh['row_0'=2,'row_1'=4,'col_0'=2,'col_1'=4,'col_2'=2] {'row_1'}, use_global_device_ids=true, to_apply=%region_73.0 | all-reduce | flops 4 | bytes 32 | tf_op jit(solution)/shard_map/psum | solution.py:15
  456.1 6.0 %psum.438 = f32[2,2]{1,0:T(2,128)S(1)} all-reduce(f32[2,2]{1,0:T(2,128)S(1)} %psum.437), channel_id=1, replica_groups=mesh['row_0'=2,'row_1'=4,'col_0'=2,'col_1'=4,'col_2'=2] {'col_1'}, use_global_device_ids=true, to_apply=%region_75.0 | all-reduce | flops 4 | bytes 32 | tf_op jit(solution)/shard_map/psum | solution.py:15
  462.1 8.4 %psum.439 = f32[2,2]{1,0:T(2,128)S(1)} all-reduce(f32[2,2]{1,0:T(2,128)S(1)} %psum.438), channel_id=1, replica_groups=mesh['row_0'=2,'row_1'=4,'col_0'=2,'col_1'=4,'col_2'=2] {'col_2'}, use_global_device_ids=true, to_apply=%region_76.0 | all-reduce | flops 4 | bytes 32 | tf_op jit(solution)/shard_map/psum | solution.py:15
  (220 shorter events, 224.8 us)
Async XLA Ops:
  1.4 33.8 %collective-permute-start.1 = (f32[2,6,256]{2,1,0:T(8,128)S(1)}, f32[2,6,256]{2,1,0:T(8,128)S(1)}, u32[]{:S(2)}, u32[]{:S(2)}) collective-permute-start(f32[2,6,256]{2,1,0:T(8,128)S(1)} %get-tuple-element.87), channel_id=1, source_target_pairs={{16,0},{32,16},{48,32},{64,48},{80,64},{96,80},{112,96},{0,112},{1... | collective-permute-start | bytes 36872 | tf_op jit(solution)/shard_map/ppermute | solution.py:28
  8.4 26.7 %collective-permute-start = (f32[2,6,256]{2,1,0:T(8,128)S(1)}, f32[2,6,256]{2,1,0:T(8,128)S(1)}, u32[]{:S(2)}, u32[]{:S(2)}) collective-permute-start(f32[2,6,256]{2,1,0:T(8,128)S(1)} %get-tuple-element.86), channel_id=1, source_target_pairs={{0,16},{16,32},{32,48},{48,64},{64,80},{80,96},{96,112},{112,0},{1... | collective-permute-start | bytes 36872 | tf_op jit(solution)/shard_map/ppermute | solution.py:26
  9.5 12.9 %collective-permute-start.13 = (f32[5,256]{1,0:T(8,128)S(1)}, f32[5,256]{1,0:T(8,128)S(1)}, u32[]{:S(2)}, u32[]{:S(2)}) collective-permute-start(f32[5,256]{1,0:T(8,128)S(1)} %get-tuple-element.95), channel_id=1, source_target_pairs={{16,0},{32,16},{48,32},{64,48},{80,64},{96,80},{112,96},{0,112},{1... | collective-permute-start | bytes 15368 | tf_op jit(solution)/shard_map/ppermute | solution.py:28
  14.6 2.6 collective-permute-start.9
  14.7 6.2 %collective-permute-start.8 = (f32[5,256]{1,0:T(8,128)S(1)}, f32[5,256]{1,0:T(8,128)S(1)}, u32[]{:S(2)}, u32[]{:S(2)}) collective-permute-start(f32[5,256]{1,0:T(8,128)S(1)} %get-tuple-element.92), channel_id=1, source_target_pairs={{0,16},{16,32},{32,48},{48,64},{64,80},{80,96},{96,112},{112,0},{1... | collective-permute-start | bytes 15368 | tf_op jit(solution)/shard_map/ppermute | solution.py:26
  17.1 8.5 %collective-permute-start.12 = (f32[5,256]{1,0:T(8,128)S(1)}, f32[5,256]{1,0:T(8,128)S(1)}, u32[]{:S(2)}, u32[]{:S(2)}) collective-permute-start(f32[5,256]{1,0:T(8,128)S(1)} %get-tuple-element.94), channel_id=1, source_target_pairs={{0,16},{16,32},{32,48},{48,64},{64,80},{80,96},{96,112},{112,0},{1... | collective-permute-start | bytes 15368 | tf_op jit(solution)/shard_map/ppermute | solution.py:26
  20.8 20.1 %collective-permute-start.5 = (f32[2,6,256]{2,1,0:T(8,128)S(1)}, f32[2,6,256]{2,1,0:T(8,128)S(1)}, u32[]{:S(2)}, u32[]{:S(2)}) collective-permute-start(f32[2,6,256]{2,1,0:T(8,128)S(1)} %get-tuple-element.85), channel_id=1, source_target_pairs={{16,0},{32,16},{48,32},{64,48},{80,64},{96,80},{112,96},{0,112},{1... | collective-permute-start | bytes 36872 | tf_op jit(solution)/shard_map/ppermute | solution.py:28
  22.4 7.2 %collective-permute-start.11 = (f32[266,5]{1,0:T(8,128)S(1)}, f32[266,5]{1,0:T(8,128)S(1)}, u32[]{:S(2)}, u32[]{:S(2)}) collective-permute-start(f32[266,5]{1,0:T(8,128)S(1)} %get-tuple-element.89), channel_id=1, source_target_pairs={{1,0},{2,1},{3,2},{4,3},{5,4},{6,5},{7,6},{8,7},{9,8},{10,9},{11,1... | collective-permute-start | bytes 15968 | tf_op jit(solution)/shard_map/ppermute | solution.py:28
  25.7 4.6 collective-permute-start.10
  29.6 4.5 collective-permute-start.15
  30.3 4.5 collective-permute-start.14
  34.1 6.9 %collective-permute-start.4 = (f32[2,6,256]{2,1,0:T(8,128)S(1)}, f32[2,6,256]{2,1,0:T(8,128)S(1)}, u32[]{:S(2)}, u32[]{:S(2)}) collective-permute-start(f32[2,6,256]{2,1,0:T(8,128)S(1)} %get-tuple-element.84), channel_id=1, source_target_pairs={{0,16},{16,32},{32,48},{48,64},{64,80},{80,96},{96,112},{112,0},{1... | collective-permute-start | bytes 36872 | tf_op jit(solution)/shard_map/ppermute | solution.py:26
  35.4 7.6 %collective-permute-start.3 = (f32[2,268,6]{2,1,0:T(8,128)S(1)}, f32[2,268,6]{2,1,0:T(8,128)S(1)}, u32[]{:S(2)}, u32[]{:S(2)}) collective-permute-start(f32[2,268,6]{2,1,0:T(8,128)S(1)} %get-tuple-element.81), channel_id=1, source_target_pairs={{1,0},{2,1},{3,2},{4,3},{5,4},{6,5},{7,6},{8,7},{9,8},{10,9},{11,1... | collective-permute-start | bytes 38600 | tf_op jit(solution)/shard_map/ppermute | solution.py:28
  40.9 3.5 collective-permute-start.2
  41.1 6.3 %collective-permute-start.7 = (f32[2,268,6]{2,1,0:T(8,128)S(1)}, f32[2,268,6]{2,1,0:T(8,128)S(1)}, u32[]{:S(2)}, u32[]{:S(2)}) collective-permute-start(f32[2,268,6]{2,1,0:T(8,128)S(1)} %get-tuple-element.79), channel_id=1, source_target_pairs={{1,0},{2,1},{3,2},{4,3},{5,4},{6,5},{7,6},{8,7},{9,8},{10,9},{11,1... | collective-permute-start | bytes 38600 | tf_op jit(solution)/shard_map/ppermute | solution.py:28
  42.5 5.0 %collective-permute-start.6 = (f32[2,268,6]{2,1,0:T(8,128)S(1)}, f32[2,268,6]{2,1,0:T(8,128)S(1)}, u32[]{:S(2)}, u32[]{:S(2)}) collective-permute-start(f32[2,268,6]{2,1,0:T(8,128)S(1)} %get-tuple-element.78), channel_id=1, source_target_pairs={{0,1},{1,2},{2,3},{3,4},{4,5},{5,6},{6,7},{7,8},{8,9},{9,10},{10,1... | collective-permute-start | bytes 38600 | tf_op jit(solution)/shard_map/ppermute | solution.py:26
  270.4 11.1 %collective-permute-start.17 = (f32[2,6,256]{2,1,0:T(8,128)S(1)}, f32[2,6,256]{2,1,0:T(8,128)S(1)}, u32[]{:S(2)}, u32[]{:S(2)}) collective-permute-start(f32[2,6,256]{2,1,0:T(8,128)S(1)} %get-tuple-element.70), channel_id=1, source_target_pairs={{16,0},{32,16},{48,32},{64,48},{80,64},{96,80},{112,96},{0,112},{1... | collective-permute-start | bytes 36872 | tf_op jit(solution)/shard_map/ppermute | solution.py:28
  274.5 7.0 %collective-permute-start.16 = (f32[2,6,256]{2,1,0:T(8,128)S(1)}, f32[2,6,256]{2,1,0:T(8,128)S(1)}, u32[]{:S(2)}, u32[]{:S(2)}) collective-permute-start(f32[2,6,256]{2,1,0:T(8,128)S(1)} %get-tuple-element.69), channel_id=1, source_target_pairs={{0,16},{16,32},{32,48},{48,64},{64,80},{80,96},{96,112},{112,0},{1... | collective-permute-start | bytes 36872 | tf_op jit(solution)/shard_map/ppermute | solution.py:26
  276.3 7.2 %collective-permute-start.21 = (f32[2,6,256]{2,1,0:T(8,128)S(1)}, f32[2,6,256]{2,1,0:T(8,128)S(1)}, u32[]{:S(2)}, u32[]{:S(2)}) collective-permute-start(f32[2,6,256]{2,1,0:T(8,128)S(1)} %get-tuple-element.83), channel_id=1, source_target_pairs={{16,0},{32,16},{48,32},{64,48},{80,64},{96,80},{112,96},{0,112},{1... | collective-permute-start | bytes 36872 | tf_op jit(solution)/shard_map/ppermute | solution.py:28
  281.5 6.2 %collective-permute-start.20 = (f32[2,6,256]{2,1,0:T(8,128)S(1)}, f32[2,6,256]{2,1,0:T(8,128)S(1)}, u32[]{:S(2)}, u32[]{:S(2)}) collective-permute-start(f32[2,6,256]{2,1,0:T(8,128)S(1)} %get-tuple-element.82), channel_id=1, source_target_pairs={{0,16},{16,32},{32,48},{48,64},{64,80},{80,96},{96,112},{112,0},{1... | collective-permute-start | bytes 36872 | tf_op jit(solution)/shard_map/ppermute | solution.py:26
  281.7 8.6 %collective-permute-start.19 = (f32[2,268,6]{2,1,0:T(8,128)S(1)}, f32[2,268,6]{2,1,0:T(8,128)S(1)}, u32[]{:S(2)}, u32[]{:S(2)}) collective-permute-start(f32[2,268,6]{2,1,0:T(8,128)S(1)} %get-tuple-element.77), channel_id=1, source_target_pairs={{1,0},{2,1},{3,2},{4,3},{5,4},{6,5},{7,6},{8,7},{9,8},{10,9},{11,1... | collective-permute-start | bytes 38600 | tf_op jit(solution)/shard_map/ppermute | solution.py:28
  283.0 7.3 %collective-permute-start.18 = (f32[2,268,6]{2,1,0:T(8,128)S(1)}, f32[2,268,6]{2,1,0:T(8,128)S(1)}, u32[]{:S(2)}, u32[]{:S(2)}) collective-permute-start(f32[2,268,6]{2,1,0:T(8,128)S(1)} %get-tuple-element.76), channel_id=1, source_target_pairs={{0,1},{1,2},{2,3},{3,4},{4,5},{5,6},{6,7},{7,8},{8,9},{9,10},{10,1... | collective-permute-start | bytes 38600 | tf_op jit(solution)/shard_map/ppermute | solution.py:26
  287.9 6.2 %collective-permute-start.23 = (f32[2,268,6]{2,1,0:T(8,128)S(1)}, f32[2,268,6]{2,1,0:T(8,128)S(1)}, u32[]{:S(2)}, u32[]{:S(2)}) collective-permute-start(f32[2,268,6]{2,1,0:T(8,128)S(1)} %get-tuple-element.75), channel_id=1, source_target_pairs={{1,0},{2,1},{3,2},{4,3},{5,4},{6,5},{7,6},{8,7},{9,8},{10,9},{11,1... | collective-permute-start | bytes 38600 | tf_op jit(solution)/shard_map/ppermute | solution.py:28
  290.3 3.8 collective-permute-start.22
  297.9 33.9 %copy-start.2 = (f32[262,262]{1,0:T(8,128)S(1)}, f32[262,262]{1,0:T(8,128)}, u32[]{:S(2)}) copy-start(f32[262,262]{1,0:T(8,128)} %slice_add_fusion.38) | copy-start | bytes 823732
  297.9 33.9 %copy-start.5 = (f32[262,262]{1,0:T(8,128)S(1)}, f32[262,262]{1,0:T(8,128)}, u32[]{:S(2)}) copy-start(f32[262,262]{1,0:T(8,128)} %slice.726) | copy-start | bytes 823732
  335.3 33.6 %copy-start = (f32[260,260]{1,0:T(8,128)S(1)}, f32[260,260]{1,0:T(8,128)}, u32[]{:S(2)}) copy-start(f32[260,260]{1,0:T(8,128)} %slice_add_fusion.37) | copy-start | bytes 811204
  335.3 33.6 %copy-start.3 = (f32[260,260]{1,0:T(8,128)S(1)}, f32[260,260]{1,0:T(8,128)}, u32[]{:S(2)}) copy-start(f32[260,260]{1,0:T(8,128)} %slice.738) | copy-start | bytes 811204
  406.0 33.6 %copy-start.11 = (f32[256,256]{1,0:T(8,128)S(1)}, f32[256,256]{1,0:T(8,128)}, u32[]{:S(2)}) copy-start(f32[256,256]{1,0:T(8,128)} %copy-done.10) | copy-start | bytes 786436
  439.6 30.9 %copy-start.19 = (f32[2,2]{1,0:T(2,128)}, f32[2,2]{1,0:T(2,128)S(1)}, u32[]{:S(2)}) copy-start(f32[2,2]{1,0:T(2,128)S(1)} %get-tuple-element.10) | copy-start | bytes 52
  439.6 31.4 %copy-start.14 = (f32[2,258,258]{2,1,0:T(8,128)S(1)}, f32[2,258,258]{2,1,0:T(8,128)}, u32[]{:S(2)}) copy-start(f32[2,258,258]{2,1,0:T(8,128)} %get-tuple-element.13) | copy-start | bytes 1597540
  441.0 32.1 %copy-start.15 = (f32[2,256,256]{2,1,0:T(8,128)}, f32[2,256,256]{2,1,0:T(8,128)S(1)}, u32[]{:S(2)}) copy-start(f32[2,256,256]{2,1,0:T(8,128)S(1)} %get-tuple-element.9) | copy-start | bytes 1572868
  (12 other events, 98.3 us)
where the time goes:
time: 482 us; the launch traced here: 473 us
  blocking collectives  352 us (73%)
  other arithmetic  49.2 us (10%)
  starting transfers between devices  44.4 us (9%)
  waiting for transfers between devices  19.4 us (4%)
  local copies, waits for them, and re-layouts  7.03 us (1%)
    psum x55, blocking collectives, over_axes(): x = lax.psum(x, axis)  352 us
    ppermute x12, starting transfers between devices, padded(): lax.ppermute(head, axis, [((i + 1) % count, i) for i in range(count)])  36.7 us
    add x10, other arithmetic, shards(): field = field + size_grid * moment  28.9 us
    ppermute x12, waiting for transfers between devices, padded(): lax.ppermute(tail, axis, [(i, (i + 1) % count) for i in range(count)])  10.7 us
  transfers between devices with their start and end apart: 24, of which 10 were waited for; matrix products, arithmetic and copies ran while one was open for 1% of the time, Pallas kernels for 0%

commit v1 on v0

v1 whole, which is shorter than its diff:
```python
import functools

import jax
import jax.numpy as jnp
from jax import lax
from jax.experimental import pallas as pl
from jax.experimental.pallas import tpu as pltpu
from jax.sharding import Mesh
from jax.sharding import PartitionSpec as P

STEPS = 10
ALL = ("row_0", "row_1", "col_0", "col_1", "col_2")
ROW = ("row_0", "row_1")
COL = ("col_0", "col_1", "col_2")

SIZE = 256
HALO = 16
GUARD = 8
TOP = GUARD + HALO
ROWS = 2 * TOP + SIZE
END = TOP + SIZE
FIELDS = 6
SHIFT = 8.0
VMEM = pl.BlockSpec(memory_space=pltpu.VMEM)
ANY = pl.BlockSpec(memory_space=pl.ANY)
F32 = jnp.float32
UNROLL = 2


def lanes():
    return lax.broadcasted_iota(jnp.int32, (8, 128), 1)


def splat(pair, chain):
    return jnp.broadcast_to(pair[:, chain : chain + 1], (8, 128))


def shifted(tiles, lane):
    right = [pltpu.roll(t, 127, 1) for t in tiles]
    left = [pltpu.roll(t, 1, 1) for t in tiles]
    last, first = lane == 127, lane == 0
    return [
        jnp.where(last, right[(i + 1) % 3], right[i]) + jnp.where(first, left[(i + 2) % 3], left[i])
        for i in range(3)
    ]


def applied(field, kappa, chain, row, lane, tiles):
    center = [field[chain, i, pl.ds(row, 8), :] for i in range(3)]
    beside = shifted(center, lane)
    result = []
    for i in range(tiles):
        around = beside[i] + (
            field[chain, i, pl.ds(row - 1, 8), :] + field[chain, i, pl.ds(row + 1, 8), :]
        )
        result.append((kappa[i, pl.ds(row, 8), :] + 4.0) * center[i] - around)
    return center, result


def loop(start, stop, body, init):
    def step(i, carry):
        return body(pl.multiple_of(start + 8 * i, 8), carry)

    return lax.fori_loop(0, (stop - start) // 8, step, init, unroll=UNROLL)


def advance(source, target, moment, counts, kappa, offset, tau, size, first_scale, sums):
    lane = lanes()
    offsets = [splat(offset, c) for c in range(2)]
    taus = [splat(tau, c) for c in range(2)]
    sizes = [splat(size, c) for c in range(2)]
    kicks = [first_scale * s for s in sizes]

    def body(row, carry, with_sums):
        carry = list(carry)
        count = [counts[i, pl.ds(row, 8), :] for i in range(3)]
        for c in range(2):
            center, result = applied(source, kappa, c, row, lane, 3)
            for i in range(3):
                intensity = jnp.exp(offsets[c] + center[i])
                gradient = taus[c] * result[i] - count[i] + intensity
                value = moment[c, i, pl.ds(row, 8), :] - kicks[c] * gradient
                moment[c, i, pl.ds(row, 8), :] = value
                target[c, i, pl.ds(row, 8), :] = center[i] + sizes[c] * value
                if with_sums and i < 2:
                    carry[c] += center[i] * result[i]
                    carry[2 + c] += intensity
        return tuple(carry)

    halo = functools.partial(body, with_sums=False)
    loop(GUARD, TOP, halo, ())
    loop(END, ROWS - GUARD, halo, ())
    if not sums:
        loop(TOP, END, halo, ())
        return None
    return loop(
        TOP, END, functools.partial(body, with_sums=True), (jnp.zeros((8, 128), F32),) * 4
    )


def sums_of(field, kappa, lead):
    lane = lanes()
    leads = [splat(lead, c) for c in range(2)]

    def body(row, carry):
        carry = list(carry)
        for c in range(2):
            center, result = applied(field, kappa, c, row, lane, 2)
            for i in range(2):
                carry[c] += center[i] * result[i]
                carry[2 + c] += jnp.exp(leads[c] + center[i])
        return tuple(carry)

    return loop(TOP, END, body, (jnp.zeros((8, 128), F32),) * 4)


def put_sums(out, values):
    lane = lax.broadcasted_iota(jnp.int32, (1, 8), 1)
    row = jnp.zeros((1, 8), F32)
    for i, value in enumerate(values):
        total = jnp.sum(jnp.sum(value, axis=0, keepdims=True), axis=1, keepdims=True)
        row = jnp.where(lane == i, total, row)
    out[...] = row


def start_kernel(
    latent, momentum, counts_in, kappa_in, offset,
    field, moment, counts, kappa, left, right, partial, raw, sems,
):
    copies = []
    for i in range(2):
        cols = pl.ds(128 * i, 128)
        own = pl.ds(TOP, SIZE)
        for c in range(2):
            copies.append((latent.at[c, :, cols], field.at[c, i, own, :]))
            copies.append((momentum.at[c, :, cols], moment.at[c, i, own, :]))
        copies.append((counts_in.at[:, cols], raw.at[i]))
        copies.append((kappa_in.at[:, cols], kappa.at[i, own, :]))
    copies = [pltpu.make_async_copy(a, b, sems.at[n]) for n, (a, b) in enumerate(copies)]
    for copy in copies:
        copy.start()
    for copy in copies:
        copy.wait()
    lane = lanes()
    group = lane // HALO
    offsets = [splat(offset[...], c) for c in range(2)]

    def body(row, carry):
        carry = list(carry)
        here = row - TOP
        for i in range(2):
            count = raw[i, pl.ds(pl.multiple_of(here, 8), 8), :].astype(F32)
            counts[i, pl.ds(row, 8), :] = count
            carry[4] += count
        for c in range(2):
            tiles = [field[c, i, pl.ds(row, 8), :] for i in range(2)]
            right0 = pltpu.roll(tiles[0], 127, 1)
            right1 = pltpu.roll(tiles[1], 127, 1)
            beside = [jnp.where(lane == 127, right1, right0), jnp.where(lane == 127, 0.0, right1)]
            for i in range(2):
                below = field[c, i, pl.ds(row + 1, 8), :]
                inside = lax.broadcasted_iota(jnp.int32, (8, 128), 0) + row < END - 1
                below = jnp.where(inside, below, 0.0)
                weight = (kappa[i, pl.ds(row, 8), :] + 4.0) * tiles[i]
                carry[c] += tiles[i] * (weight - 2.0 * (beside[i] + below))
                carry[2 + c] += jnp.exp(offsets[c] + tiles[i])
        for out, tile, base in ((left, 0, 0), (right, 1, HALO)):
            parts = [
                field[0, tile, pl.ds(row, 8), :],
                field[1, tile, pl.ds(row, 8), :],
                moment[0, tile, pl.ds(row, 8), :],
                moment[1, tile, pl.ds(row, 8), :],
                counts[tile, pl.ds(row, 8), :],
                kappa[tile, pl.ds(row, 8), :],
            ]
            packed = jnp.zeros((8, 128), F32)
            for n, part in enumerate(parts):
                shift = (HALO * n + base) % 128
                moved = part if shift == 0 else pltpu.roll(part, shift, 1)
                packed = jnp.where(group == n, moved, packed)
            out[pl.ds(pl.multiple_of(here, 8), 8), :] = packed
        return tuple(carry)

    totals = loop(TOP, END, body, (jnp.zeros((8, 128), F32),) * 5)
    put_sums(partial, totals)


def unpack(buffers, lane, n):
    from_right, from_left = buffers
    near = HALO * n % 128
    far = (HALO * n + HALO) % 128
    a = from_right if near == 0 else pltpu.roll(from_right, 128 - near, 1)
    b = from_left if far == 0 else pltpu.roll(from_left, 128 - far, 1)
    return jnp.where(lane < HALO, a, jnp.where(lane >= 128 - HALO, b, 0.0))


def parts_of(field, moment, counts, kappa):
    return [field.at[0], field.at[1], moment.at[0], moment.at[1], counts, kappa]


def columns_kernel(
    field_in, moment_in, counts_in, kappa_in, from_right, from_left, below, partial_in,
    field, moment, counts, kappa, up, down, partial,
):
    del field_in, moment_in, counts_in, kappa_in
    lane = lanes()
    parts = parts_of(field, moment, counts, kappa)

    def body(row, carry):
        carry = list(carry)
        here = pl.ds(pl.multiple_of(row - TOP, 8), 8)
        buffers = (from_right[here, :], from_left[here, :])
        for n, part in enumerate(parts):
            tile = unpack(buffers, lane, n)
            part[2, pl.ds(row, 8), :] = tile
            if n < 2:
                edge = pltpu.roll(part[1, pl.ds(row, 8), :], 1, 1) * tile
                carry[n] += jnp.where(lane == 0, edge, 0.0)
        return tuple(carry)

    edges = loop(TOP, END, body, (jnp.zeros((8, 128), F32),) * 2)
    for out, row, here in ((up, TOP, 0), (down, END - HALO, SIZE - HALO)):
        for n, part in enumerate(parts):
            for i in range(2):
                out[pl.ds(HALO * n, HALO), pl.ds(128 * i, 128)] = part[i, pl.ds(row, HALO), :]
        corner = pl.ds(HALO * FIELDS, HALO)
        out[corner, pl.ds(0, 128)] = from_right[pl.ds(here, HALO), :]
        out[corner, pl.ds(128, 128)] = from_left[pl.ds(here, HALO), :]
    totals = []
    for c in range(2):
        total = jnp.sum(jnp.sum(edges[c], axis=0, keepdims=True), axis=1, keepdims=True)
        for i in range(2):
            own = field[c, i, pl.ds(END - 1, 1), :]
            other = below[pl.ds(c, 1), pl.ds(128 * i, 128)]
            total += jnp.sum(own * other, axis=1, keepdims=True)
        totals.append(total)
    index = lax.broadcasted_iota(jnp.int32, (1, 8), 1)
    extra = jnp.where(index == 0, totals[0], jnp.where(index == 1, totals[1], 0.0))
    partial[...] = partial_in[...] - 2.0 * extra


def unpack_rows(from_above, from_below, field, moment, counts, kappa):
    lane = lanes()
    parts = parts_of(field, moment, counts, kappa)
    for buffer, row in ((from_above, GUARD), (from_below, END)):
        for block in range(0, HALO, 8):
            corner = pl.ds(HALO * FIELDS + block, 8)
            buffers = (buffer[corner, pl.ds(0, 128)], buffer[corner, pl.ds(128, 128)])
            for n, part in enumerate(parts):
                for i in range(2):
                    part[i, pl.ds(row + block, 8), :] = buffer[
                        pl.ds(HALO * n + block, 8), pl.ds(128 * i, 128)
                    ]
                part[2, pl.ds(row + block, 8), :] = unpack(buffers, lane, n)


OFFSET, SCALE, SPEED_0, SPEED_1, STEP, COUNT = range(6)


def read_table(table):
    return [table[pl.ds(i, 1), pl.ds(0, 2)] for i in range(6)]


def write_table(out, rows):
    out[...] = jnp.zeros((8, 128), F32)
    for i, row in enumerate(rows):
        out[pl.ds(i, 1), pl.ds(0, 2)] = row


def accel_of(quadratic, intensity, scale, count, total):
    return (intensity / total - count, 0.5 * jnp.exp(scale) * quadratic / total - 0.5)


def first_step_kernel(
    total, table, reduced, from_above, from_below, field_in, moment_in, counts_in, kappa_in,
    table_out, field, moment, counts, kappa, partial, other,
):
    del field_in, moment_in, counts_in, kappa_in
    unpack_rows(from_above, from_below, field, moment, counts, kappa)
    offset, scale, speed_0, speed_1, size, _ = read_table(table)
    quadratic, intensity = reduced[:, 0:2], reduced[:, 2:4]
    count = jnp.broadcast_to(reduced[:, 4:5], (1, 2)) / total
    a_0, a_1 = accel_of(quadratic, intensity, scale, count, total)
    advance(field, other, moment, counts, kappa, offset, jnp.exp(scale), size, 0.5, False)
    speed_0, speed_1 = speed_0 - 0.5 * size * a_0, speed_1 - 0.5 * size * a_1
    offset, scale = offset + size * speed_0, scale + size * speed_1
    near = advance(other, field, moment, counts, kappa, offset, jnp.exp(scale), size, 1.0, True)
    far = sums_of(field, kappa, offset - SHIFT)
    put_sums(partial, (*near, *far))
    write_table(table_out, (offset, scale, speed_0, speed_1, size, count))


def two_params(table, reduced, total):
    offset, scale, speed_0, speed_1, size, count = read_table(table)
    before = offset
    a_0, a_1 = accel_of(reduced[:, 0:2], reduced[:, 2:4], scale, count, total)
    speed_0, speed_1 = speed_0 - size * a_0, speed_1 - size * a_1
    offset, scale = offset + size * speed_0, scale + size * speed_1
    intensity = reduced[:, 6:8] * jnp.exp(offset - before + SHIFT)
    a_0, a_1 = accel_of(reduced[:, 4:6], intensity, scale, count, total)
    return offset, scale, speed_0, speed_1, size, count, a_0, a_1


def two_steps_kernel(
    total, table, reduced, field_in, moment_in, counts, kappa,
    table_out, field, moment, partial, other,
):
    del field_in, moment_in
    offset, scale, speed_0, speed_1, size, count, a_0, a_1 = two_params(table, reduced, total)
    advance(field, other, moment, counts, kappa, offset, jnp.exp(scale), size, 1.0, False)
    speed_0, speed_1 = speed_0 - size * a_0, speed_1 - size * a_1
    offset, scale = offset + size * speed_0, scale + size * speed_1
    near = advance(other, field, moment, counts, kappa, offset, jnp.exp(scale), size, 1.0, True)
    far = sums_of(field, kappa, offset - SHIFT)
    put_sums(partial, (*near, *far))
    write_table(table_out, (offset, scale, speed_0, speed_1, size, count))


def last_kernel(
    total, table, reduced, field, moment, counts, kappa,
    latent_out, momentum_out, hyper_out, velocity_out, result, sems,
):
    copies = []
    for c in range(2):
        for i in range(2):
            cols = pl.ds(128 * i, 128)
            copies.append((field.at[c, i, pl.ds(TOP, SIZE), :], latent_out.at[c, :, cols]))
    for c in range(2):
        for i in range(2):
            cols = pl.ds(128 * i, 128)
            copies.append((result.at[c, i], momentum_out.at[c, :, cols]))
    copies = [pltpu.make_async_copy(a, b, sems.at[n]) for n, (a, b) in enumerate(copies)]
    for copy in copies[:4]:
        copy.start()
    offset, scale, speed_0, speed_1, size, _, a_0, a_1 = two_params(table, reduced, total)
    lane = lanes()
    tau = jnp.exp(scale)
    for c in range(2):
        offset_c, tau_c, half = splat(offset, c), splat(tau, c), 0.5 * splat(size, c)

        def body(row, carry, c=c, offset_c=offset_c, tau_c=tau_c, half=half):
            center, applied_c = applied(field, kappa, c, row, lane, 2)
            here = pl.ds(pl.multiple_of(row - TOP, 8), 8)
            for i in range(2):
                gradient = tau_c * applied_c[i] - counts[i, pl.ds(row, 8), :]
                gradient += jnp.exp(offset_c + center[i])
                result[c, i, here, :] = moment[c, i, pl.ds(row, 8), :] - half * gradient
            return carry

        loop(TOP, END, body, ())
        for copy in copies[4 + 2 * c : 6 + 2 * c]:
            copy.start()
    hyper_out[pl.ds(0, 1), :] = offset
    hyper_out[pl.ds(1, 1), :] = scale
    velocity_out[pl.ds(0, 1), :] = speed_0 - 0.5 * size * a_0
    velocity_out[pl.ds(1, 1), :] = speed_1 - 0.5 * size * a_1
    for copy in copies:
        copy.wait()


def vmem(*shape):
    return pltpu.VMEM(shape, F32)


def held(*arrays):
    return tuple(pltpu.with_memory_space_constraint(a, pltpu.VMEM) for a in arrays)


STATE = (vmem(2, 3, ROWS, 128), vmem(2, 3, ROWS, 128), vmem(3, ROWS, 128), vmem(3, ROWS, 128))
PARAMS = pltpu.CompilerParams(vmem_limit_bytes=32 << 20)


def ring(x, axes, step):
    count = lax.axis_size(axes)
    return lax.ppermute(x, axes, [(i, (i + step) % count) for i in range(count)])


def all_sum(partial):
    count = lax.axis_size(ALL)
    spread = jnp.broadcast_to(partial[None], (count,) + partial.shape)
    return jnp.sum(lax.all_to_all(spread, ALL, 0, 0, tiled=True), axis=0)


def shards(latent, momentum, hyper_params, velocity, step_size, counts, kappa_field):
    total = float(latent.shape[1] * latent.shape[2] * lax.axis_size(ALL))
    below = ring(latent[:, 0, :], ROW, -1)
    table = jnp.zeros((8, 128), F32)
    rows = jnp.concatenate([hyper_params, velocity, step_size[None]], axis=0)
    table = lax.dynamic_update_slice(table, rows, (0, 0))
    buffer = jax.ShapeDtypeStruct((SIZE, 128), F32)
    small = jax.ShapeDtypeStruct((1, 8), F32)
    field, moment, count, kappa, left, right, partial = pl.pallas_call(
        start_kernel,
        out_shape=(*STATE, buffer, buffer, small),
        in_specs=[ANY] * 4 + [VMEM],
        out_specs=(VMEM,) * 7,
        scratch_shapes=[pltpu.VMEM((2, SIZE, 128), jnp.int32), pltpu.SemaphoreType.DMA((12,))],
        compiler_params=PARAMS,
        name="start",
    )(latent, momentum, counts, kappa_field, hyper_params[0:1])
    from_right, from_left = ring(left, COL, -1), ring(right, COL, 1)
    edge = jax.ShapeDtypeStruct((HALO * (FIELDS + 1), SIZE), F32)
    field, moment, count, kappa, up, down, partial = pl.pallas_call(
        columns_kernel,
        out_shape=(*STATE, edge, edge, small),
        in_specs=[VMEM] * 8,
        out_specs=(VMEM,) * 7,
        input_output_aliases={0: 0, 1: 1, 2: 2, 3: 3},
        compiler_params=PARAMS,
        name="columns",
    )(*held(field, moment, count, kappa), from_right, from_left, below, partial)
    from_below, from_above = ring(up, ROW, -1), ring(down, ROW, 1)
    reduced = all_sum(partial)
    small_table = jax.ShapeDtypeStruct((8, 128), F32)
    table, field, moment, count, kappa, partial = pl.pallas_call(
        functools.partial(first_step_kernel, total),
        out_shape=(small_table, *STATE, small),
        in_specs=[VMEM] * 8,
        out_specs=(VMEM,) * 6,
        input_output_aliases={4: 1, 5: 2, 6: 3, 7: 4},
        scratch_shapes=[vmem(2, 3, ROWS, 128)],
        compiler_params=PARAMS,
        name="first_steps",
    )(table, reduced, from_above, from_below, *held(field, moment, count, kappa))
    for _ in range(STEPS // 2 - 1):
        reduced = all_sum(partial)
        table, field, moment, partial = pl.pallas_call(
            functools.partial(two_steps_kernel, total),
            out_shape=(small_table, *STATE[:2], small),
            in_specs=[VMEM] * 6,
            out_specs=(VMEM,) * 4,
            input_output_aliases={2: 1, 3: 2},
            scratch_shapes=[vmem(2, 3, ROWS, 128)],
            compiler_params=PARAMS,
            name="two_steps",
        )(table, reduced, *held(field, moment, count, kappa))
    reduced = all_sum(partial)
    return pl.pallas_call(
        functools.partial(last_kernel, total),
        out_shape=(
            jax.ShapeDtypeStruct(latent.shape, F32),
            jax.ShapeDtypeStruct(latent.shape, F32),
            jax.ShapeDtypeStruct((2, 2), F32),
            jax.ShapeDtypeStruct((2, 2), F32),
        ),
        in_specs=[VMEM] * 6,
        out_specs=(ANY, ANY, VMEM, VMEM),
        scratch_shapes=[vmem(2, 2, SIZE, 128), pltpu.SemaphoreType.DMA((8,))],
        compiler_params=PARAMS,
        name="last",
    )(table, reduced, *held(field, moment, count, kappa))


def solution(mesh):
    torus = Mesh(mesh.devices.reshape(2, 4, 2, 4, 2), ALL)
    return jax.shard_map(
        shards,
        mesh=torus,
        in_specs=(P(None, ROW, COL), P(None, ROW, COL), P(), P(), P(), P(ROW, COL), P(ROW, COL)),
        out_specs=(P(None, ROW, COL), P(None, ROW, COL), P(), P()),
        check_vma=False,
    )
```

time: 482 us -> 145 us (0.30); the launches traced: 473 us -> 144 us
  blocking collectives: 352 us -> 68.7 us
  other arithmetic: 49.2 us -> 0.92 us
  Pallas kernels: 0 us -> 36.3 us
  starting transfers between devices: 44.4 us -> 21.5 us
  waiting for transfers between devices: 19.4 us -> 9.86 us
    psum x55 -> x0, blocking collectives: 352 us -> none  [over_axes(): x = lax.psum(x, axis)]
    all_to_all x0 -> x5, blocking collectives: none -> 68.7 us  [all_sum(): return jnp.sum(lax.all_to_all(spread, ALL, 0, 0, tiled=True), axis=0)]
    pallas_call x0 -> x8, Pallas kernels: none -> 36.3 us  [the longest x4 22.7 us: shards(): pl.pallas_call(functools.partial(two_steps_kernel, total), out_shape=(sma...]
    add x26 -> x0, other arithmetic: 33 us -> none  [the longest x10 28.9 us: shards(): field = field + size_grid * moment]
    ppermute x24 -> x5, starting transfers between devices: 44.4 us -> 14.5 us  [ring(): lax.ppermute(x, axes, [(i, (i + step) % count) for i in range(count)])]
    ppermute x24 -> x5, waiting for transfers between devices: 19.4 us -> 0.75 us  [ring(): lax.ppermute(x, axes, [(i, (i + step) % count) for i in range(count)])]
    all_to_all x0 -> x1, waiting for transfers between devices: none -> 9.12 us  [all_sum(): return jnp.sum(lax.all_to_all(spread, ALL, 0, 0, tiled=True), axis=0)]
    reduce_sum x19 -> x6, other arithmetic: 9.41 us -> 0.91 us  [all_sum(): return jnp.sum(lax.all_to_all(spread, ALL, 0, 0, tiled=True), axis=0)]
  transfers between devices with their start and end apart: 24 -> 6, of which waited for: 10 -> 2; matrix products, arithmetic and copies ran while one was open for 1% -> 1% of each run, Pallas kernels for 0% -> 0%
where the time goes in v1:
time: 145 us; the launch traced here: 144 us
  blocking collectives  68.7 us (47%)
  Pallas kernels  36.3 us (25%)
  starting transfers between devices  21.5 us (15%)
  waiting for transfers between devices  9.86 us (7%)
  local copies, waits for them, and re-layouts  6.2 us (4%)
    all_to_all x5, blocking collectives, all_sum(): return jnp.sum(lax.all_to_all(spread, ALL, 0, 0, tiled=True), axis=0)  68.7 us
    pallas_call x4, Pallas kernels, shards(): pl.pallas_call(functools.partial(two_steps_kernel, total), out_shape=(sma...  22.7 us
    ppermute x5, starting transfers between devices, ring(): lax.ppermute(x, axes, [(i, (i + step) % count) for i in range(count)])  14.5 us
    all_to_all x1, waiting for transfers between devices, all_sum(): return jnp.sum(lax.all_to_all(spread, ALL, 0, 0, tiled=True), axis=0)  9.12 us
    all_to_all x1, starting transfers between devices, all_sum(): return jnp.sum(lax.all_to_all(spread, ALL, 0, 0, tiled=True), axis=0)  7.01 us
    pallas_call x1, Pallas kernels, shards(): pl.pallas_call(functools.partial(first_step_kernel, total), out_shape=(sm...  5.58 us
    unnamed x15, local copies, waits for them, and re-layouts  4.65 us
    pallas_call x1, Pallas kernels, shards(): pl.pallas_call(functools.partial(last_kernel, total), out_shape=(jax.Shap...  4.48 us
  transfers between devices with their start and end apart: 6, of which 2 were waited for; matrix products, arithmetic and copies ran while one was open for 1% of the time, Pallas kernels for 0%

profile of v1, /device:TPU:1, one launch (start us, length us, event | category | flops | bytes accessed | tf_op | source)
XLA Modules:
  0.0 144.2 jit_solution(7369423865971485392)
XLA Ops:
  0.6 0.7 slice.6.offset
  1.3 1.0 copy-done
  2.4 1.0 copy-done.1
  3.4 0.9 copy-done.2
  4.3 0.9 copy-done.3
  5.3 2.0 %start.1 = (f32[2,3,304,128]{3,2,1,0:T(8,128)S(1)}, f32[2,3,304,128]{3,2,1,0:T(8,128)S(1)}, f32[3,304,128]{2,1,0:T(8,128)S(1)}, f32[3,304,128]{2,1,0:T(8,128)S(1...) custom-call(f32[2,256,256]{2,1,0:T(8,128)S(1)} %copy-done, f32[2,256,256]{2,1,0:T(8,128)S(1)} %copy-done.1, ...), custom_call_target="tpu_custom_call" | custom-call | tf_op jit(solution)/shard_map/start/pallas_call | solution.py:392
  7.3 1.5 %collective-permute-start = (f32[256,128]{1,0:T(8,128)S(1)}, f32[256,128]{1,0:T(8,128)S(1)}, u32[]{:S(2)}, u32[]{:S(2)}) collective-permute-start(f32[256,128]{1,0:T(8,128)S(1)} %get-tuple-element.44), channel_id=1, source_target_pairs={{0,15},{1,0},{2,1},{3,2},{4,3},{5,4},{6,5},{7,6},{8,7},{9,8},{10,9... | collective-permute-start | bytes 393224 | tf_op jit(solution)/shard_map/ppermute | solution.py:375
  8.8 1.3 collective-permute-start.1
  10.1 6.2 %collective-permute-start.2 = (f32[2,256]{1,0:T(2,128)S(1)}, f32[2,256]{1,0:T(2,128)S(1)}, u32[]{:S(2)}, u32[]{:S(2)}) collective-permute-start(f32[2,256]{1,0:T(2,128)S(1)} %bitcast.28), channel_id=1, source_target_pairs={{0,112},{16,0},{32,16},{48,32},{64,48},{80,64},{96,80},{112,96},{1... | collective-permute-start | bytes 6152 | tf_op jit(solution)/shard_map/ppermute | solution.py:375
  16.3 0.7 collective-permute-done.2.below
  17.1 1.6 %columns.1 = (f32[2,3,304,128]{3,2,1,0:T(8,128)S(1)}, f32[2,3,304,128]{3,2,1,0:T(8,128)S(1)}, f32[3,304,128]{2,1,0:T(8,128)S(1)}, f32[3,304,128]{2,1,0:T(8,128)S...) custom-call(f32[2,3,304,128]{3,2,1,0:T(8,128)S(1)} %get-tuple-elemen, ...), custom_call_target="tpu_custom_call", output_to_operand_aliasing={{0}: (0, {}), {1}: (1, {}), {2}: (2, {}), {3}: (3, {})} | custom-call | tf_op jit(solution)/shard_map/columns/pallas_call | solution.py:403
  18.7 5.4 %collective-permute-start.4 = (f32[112,256]{1,0:T(8,128)S(1)}, f32[112,256]{1,0:T(8,128)S(1)}, u32[]{:S(2)}, u32[]{:S(2)}) collective-permute-start(f32[112,256]{1,0:T(8,128)S(1)} %get-tuple-element.49), channel_id=1, source_target_pairs={{0,112},{16,0},{32,16},{48,32},{64,48},{80,64},{96,80},{112,96},{1... | collective-permute-start | bytes 344072 | tf_op jit(solution)/shard_map/ppermute | solution.py:375
  24.1 0.7 broadcast_in_dim.54
  24.8 7.0 %all-to-all-start = ((f32[128,1,8]{2,1,0:T(1,128)}), f32[128,1,8]{2,1,0:T(1,128)S(1)}, u32[]{:S(2)}, u32[]{:S(2)}) async-start(f32[128,1,8]{2,1,0:T(1,128)} %broadcast_in_dim.54), calls=%async_computation | async-start | bytes 131072 | tf_op jit(solution)/shard_map/all_to_all | solution.py:381
  31.8 0.6 copy-done.4
  32.5 9.1 %all-to-all-done = f32[128,1,8]{2,1,0:T(1,128)S(1)} async-done(((f32[128,1,8]{2,1,0:T(1,128)}), f32[128,1,8]{2,1,0:T(1,128)S(1)}, u32[]{:S(2)}, u32[]{:S(2)}) %all-to-all-start) | async-done | bytes 4128 | tf_op jit(solution)/shard_map/all_to_all | solution.py:381
  41.6 0.2 reduce_sum.66
  41.8 5.6 %first_steps.1 = (f32[8,128]{1,0:T(8,128)S(1)}, f32[2,3,304,128]{3,2,1,0:T(8,128)S(1)}, f32[2,3,304,128]{3,2,1,0:T(8,128)S(1)}, f32[3,304,128]{2,1,0:T(8,128)S(1...) custom-call(f32[8,128]{1,0:T(8,128)S(1)} %select_maximum_fusion.tabl, ...), custom_call_target="tpu_custom_call", output_to_operand_aliasing={{1}: (4, {}), {2}: (5, {}), {3}: (6, {}), {4}: (7, {})} | custom-call | tf_op jit(solution)/shard_map/first_steps/pallas_call | solution.py:415
  47.4 13.7 %all_to_all.30 = f32[128,1,8]{2,1,0:T(1,128)S(1)} all-to-all(f32[128,1,8]{2,1,0:T(1,128)S(1)} %broadcast_in_dim.56), channel_id=1, replica_groups=mesh['row_0'=2,'row_1'=4,'col_0'=2,'col_1'=4,'col_2'=2] {'row_0','row_1'..., dimensions={0} | all-to-all | bytes 8192 | tf_op jit(solution)/shard_map/all_to_all | solution.py:381
  61.1 0.2 reduce_sum.68
  61.3 5.7 %two_steps.4 = (f32[8,128]{1,0:T(8,128)S(1)}, f32[2,3,304,128]{3,2,1,0:T(8,128)S(1)}, f32[2,3,304,128]{3,2,1,0:T(8,128)S(1)}, f32[1,8]{1,0:T(1,128)S(1)}) custom-call(f32[8,128]{1,0:T(8,128)S(1)} %get-tuple-element.54.table, f32[1,8]{1,0:T(1,128)S(1)} %bitcast.18, ...), custom_call_target="tpu_custom_call", output_to_operand_aliasing={{1}: (2, {}), {2}: (3, {})} | custom-call | tf_op jit(solution)/shard_map/two_steps/pallas_call | solution.py:427
  67.0 13.7 %all_to_all.31 = f32[128,1,8]{2,1,0:T(1,128)S(1)} all-to-all(f32[128,1,8]{2,1,0:T(1,128)S(1)} %broadcast_in_dim.58), channel_id=1, replica_groups=mesh['row_0'=2,'row_1'=4,'col_0'=2,'col_1'=4,'col_2'=2] {'row_0','row_1'..., dimensions={0} | all-to-all | bytes 8192 | tf_op jit(solution)/shard_map/all_to_all | solution.py:381
  80.8 0.2 reduce_sum.70
  80.9 5.7 %two_steps.5 = (f32[8,128]{1,0:T(8,128)S(1)}, f32[2,3,304,128]{3,2,1,0:T(8,128)S(1)}, f32[2,3,304,128]{3,2,1,0:T(8,128)S(1)}, f32[1,8]{1,0:T(1,128)S(1)}) custom-call(f32[8,128]{1,0:T(8,128)S(1)} %get-tuple-element.60.table, f32[1,8]{1,0:T(1,128)S(1)} %bitcast.19, ...), custom_call_target="tpu_custom_call", output_to_operand_aliasing={{1}: (2, {}), {2}: (3, {})} | custom-call | tf_op jit(solution)/shard_map/two_steps/pallas_call | solution.py:427
  86.6 13.7 %all_to_all.32 = f32[128,1,8]{2,1,0:T(1,128)S(1)} all-to-all(f32[128,1,8]{2,1,0:T(1,128)S(1)} %broadcast_in_dim.60), channel_id=1, replica_groups=mesh['row_0'=2,'row_1'=4,'col_0'=2,'col_1'=4,'col_2'=2] {'row_0','row_1'..., dimensions={0} | all-to-all | bytes 8192 | tf_op jit(solution)/shard_map/all_to_all | solution.py:381
  100.4 0.2 reduce_sum.72
  100.5 5.7 %two_steps.6 = (f32[8,128]{1,0:T(8,128)S(1)}, f32[2,3,304,128]{3,2,1,0:T(8,128)S(1)}, f32[2,3,304,128]{3,2,1,0:T(8,128)S(1)}, f32[1,8]{1,0:T(1,128)S(1)}) custom-call(f32[8,128]{1,0:T(8,128)S(1)} %get-tuple-element.64.table, f32[1,8]{1,0:T(1,128)S(1)} %bitcast.20, ...), custom_call_target="tpu_custom_call", output_to_operand_aliasing={{1}: (2, {}), {2}: (3, {})} | custom-call | tf_op jit(solution)/shard_map/two_steps/pallas_call | solution.py:427
  106.2 13.7 %all_to_all.33 = f32[128,1,8]{2,1,0:T(1,128)S(1)} all-to-all(f32[128,1,8]{2,1,0:T(1,128)S(1)} %broadcast_in_dim.62), channel_id=1, replica_groups=mesh['row_0'=2,'row_1'=4,'col_0'=2,'col_1'=4,'col_2'=2] {'row_0','row_1'..., dimensions={0} | all-to-all | bytes 8192 | tf_op jit(solution)/shard_map/all_to_all | solution.py:381
  120.0 0.2 reduce_sum.74
  120.1 5.7 %two_steps.7 = (f32[8,128]{1,0:T(8,128)S(1)}, f32[2,3,304,128]{3,2,1,0:T(8,128)S(1)}, f32[2,3,304,128]{3,2,1,0:T(8,128)S(1)}, f32[1,8]{1,0:T(1,128)S(1)}) custom-call(f32[8,128]{1,0:T(8,128)S(1)} %get-tuple-element.68.table, f32[1,8]{1,0:T(1,128)S(1)} %bitcast.21, ...), custom_call_target="tpu_custom_call", output_to_operand_aliasing={{1}: (2, {}), {2}: (3, {})} | custom-call | tf_op jit(solution)/shard_map/two_steps/pallas_call | solution.py:427
  125.9 13.7 %all_to_all.34 = f32[128,1,8]{2,1,0:T(1,128)S(1)} all-to-all(f32[128,1,8]{2,1,0:T(1,128)S(1)} %broadcast_in_dim.64), channel_id=1, replica_groups=mesh['row_0'=2,'row_1'=4,'col_0'=2,'col_1'=4,'col_2'=2] {'row_0','row_1'..., dimensions={0} | all-to-all | bytes 8192 | tf_op jit(solution)/shard_map/all_to_all | solution.py:381
  139.7 4.5 %last.1 = (f32[2,256,256]{2,1,0:T(8,128)}, f32[2,256,256]{2,1,0:T(8,128)}, f32[2,2]{1,0:T(2,128)}, f32[2,2]{1,0:T(2,128)}) custom-call(f32[8,128]{1,0:T(8,128)S(1)} %get-tuple-element.72.table, f32[1,8]{1,0:T(1,128)S(1)} %bitcast.17, f32[2,3,304,128]{3,2,1,0:T(8,128)S(1)} %get-tuple-element.74.field, f32[2,3,304,128]{3,2,1,0:T(8,128)S(1)} %get-tuple-element.75.moment, ...), custom_call_target="tpu_custom_call" | custom-call | tf_op jit(solution)/shard_map/last/pallas_call | solution.py:438
  (23 shorter events, 0.4 us)
Async XLA Ops:
  1.3 1.0 copy-start
  2.4 1.0 copy-start.1
  3.4 0.9 copy-start.2
  4.3 0.9 copy-start.3
  7.3 9.8 %collective-permute-start = (f32[256,128]{1,0:T(8,128)S(1)}, f32[256,128]{1,0:T(8,128)S(1)}, u32[]{:S(2)}, u32[]{:S(2)}) collective-permute-start(f32[256,128]{1,0:T(8,128)S(1)} %get-tuple-element.44), channel_id=1, source_target_pairs={{0,15},{1,0},{2,1},{3,2},{4,3},{5,4},{6,5},{7,6},{8,7},{9,8},{10,9... | collective-permute-start | bytes 393224 | tf_op jit(solution)/shard_map/ppermute | solution.py:375
  8.8 8.3 %collective-permute-start.1 = (f32[256,128]{1,0:T(8,128)S(1)}, f32[256,128]{1,0:T(8,128)S(1)}, u32[]{:S(2)}, u32[]{:S(2)}) collective-permute-start(f32[256,128]{1,0:T(8,128)S(1)} %get-tuple-element.45), channel_id=1, source_target_pairs={{0,1},{1,2},{2,3},{3,4},{4,5},{5,6},{6,7},{7,8},{8,9},{9,10},{10,1... | collective-permute-start | bytes 393224 | tf_op jit(solution)/shard_map/ppermute | solution.py:375
  10.1 7.0 %collective-permute-start.2 = (f32[2,256]{1,0:T(2,128)S(1)}, f32[2,256]{1,0:T(2,128)S(1)}, u32[]{:S(2)}, u32[]{:S(2)}) collective-permute-start(f32[2,256]{1,0:T(2,128)S(1)} %bitcast.28), channel_id=1, source_target_pairs={{0,112},{16,0},{32,16},{48,32},{64,48},{80,64},{96,80},{112,96},{1... | collective-permute-start | bytes 6152 | tf_op jit(solution)/shard_map/ppermute | solution.py:375
  18.7 23.1 %collective-permute-start.3 = (f32[112,256]{1,0:T(8,128)S(1)}, f32[112,256]{1,0:T(8,128)S(1)}, u32[]{:S(2)}, u32[]{:S(2)}) collective-permute-start(f32[112,256]{1,0:T(8,128)S(1)} %get-tuple-element.48), channel_id=1, source_target_pairs={{0,16},{16,32},{32,48},{48,64},{64,80},{80,96},{96,112},{112,0},{1... | collective-permute-start | bytes 344072 | tf_op jit(solution)/shard_map/ppermute | solution.py:375
  18.7 23.0 %collective-permute-start.4 = (f32[112,256]{1,0:T(8,128)S(1)}, f32[112,256]{1,0:T(8,128)S(1)}, u32[]{:S(2)}, u32[]{:S(2)}) collective-permute-start(f32[112,256]{1,0:T(8,128)S(1)} %get-tuple-element.49), channel_id=1, source_target_pairs={{0,112},{16,0},{32,16},{48,32},{64,48},{80,64},{96,80},{112,96},{1... | collective-permute-start | bytes 344072 | tf_op jit(solution)/shard_map/ppermute | solution.py:375
  24.8 7.0 %copy-start.5 = (f32[2,2]{1,0:T(2,128)S(1)}, f32[2,2]{1,0:T(2,128)}, u32[]{:S(2)}) copy-start(f32[2,2]{1,0:T(2,128)} %param.9) | copy-start | bytes 52
  24.8 16.8 %all-to-all-start = ((f32[128,1,8]{2,1,0:T(1,128)}), f32[128,1,8]{2,1,0:T(1,128)S(1)}, u32[]{:S(2)}, u32[]{:S(2)}) async-start(f32[128,1,8]{2,1,0:T(1,128)} %broadcast_in_dim.54), calls=%async_computation | async-start | bytes 131072 | tf_op jit(solution)/shard_map/all_to_all | solution.py:381
  31.8 0.7 copy-start.4
  31.8 0.7 copy-start.6

commit v2 on v1

v2 whole, which is shorter than its diff:
```python
import functools

import jax
import jax.numpy as jnp
from jax import lax
from jax.experimental import pallas as pl
from jax.experimental.pallas import tpu as pltpu
from jax.sharding import Mesh
from jax.sharding import PartitionSpec as P

STEPS = 10
ALL = ("row_0", "row_1", "col_0", "col_1", "col_2")
ROW = ("row_0", "row_1")
COL = ("col_0", "col_1", "col_2")

SIZE = 256
HALO = 16
GUARD = 8
TOP = GUARD + HALO
ROWS = 2 * TOP + SIZE
END = TOP + SIZE
FIELDS = 6
SHIFT = 8.0
VMEM = pl.BlockSpec(memory_space=pltpu.VMEM)
ANY = pl.BlockSpec(memory_space=pl.ANY)
F32 = jnp.float32
UNROLL = 16


def views(state):
    field, moment, slope, growth = (state.at[pl.ds(2 * i, 2)] for i in range(4))
    return field, moment, state.at[8], state.at[9], slope, growth


def lanes():
    return lax.broadcasted_iota(jnp.int32, (8, 128), 1)


def splat(pair, chain):
    return jnp.broadcast_to(pair[:, chain : chain + 1], (8, 128))


def shifted(tiles, lane):
    right = [pltpu.roll(t, 127, 1) for t in tiles]
    left = [pltpu.roll(t, 1, 1) for t in tiles]
    last, first = lane == 127, lane == 0
    return [
        jnp.where(last, right[(i + 1) % 3], right[i]) + jnp.where(first, left[(i + 2) % 3], left[i])
        for i in range(3)
    ]


def applied(field, kappa, chain, row, lane, tiles):
    center = [field[chain, i, pl.ds(row, 8), :] for i in range(3)]
    beside = shifted(center, lane)
    result = []
    for i in range(tiles):
        around = beside[i] + (
            field[chain, i, pl.ds(row - 1, 8), :] + field[chain, i, pl.ds(row + 1, 8), :]
        )
        result.append(kappa[i, pl.ds(row, 8), :] * center[i] - around)
    return center, result


def loop(start, stop, body, init):
    def step(i, carry):
        return body(pl.multiple_of(start + 8 * i, 8), carry)

    return lax.fori_loop(0, (stop - start) // 8, step, init, unroll=UNROLL)


def sweep(body, carry, depth):
    for start in (TOP - depth, END):
        loop(start, start + depth, lambda row, _: body(row, None) or (), ())
    return loop(TOP, END, body, carry)


def zeros(count):
    return (jnp.zeros((8, 128), F32),) * count


def advance(source, target, moment, counts, kappa, offset, tau, size, first_scale, depth):
    lane = lanes()
    offsets = [splat(offset, c) for c in range(2)]
    taus = [splat(tau, c) for c in range(2)]
    sizes = [splat(size, c) for c in range(2)]
    kicks = [first_scale * s for s in sizes]

    def body(row, carry):
        carry = carry and list(carry)
        count = [counts[i, pl.ds(row, 8), :] for i in range(3)]
        for c in range(2):
            center, result = applied(source, kappa, c, row, lane, 3)
            for i in range(3):
                intensity = jnp.exp(offsets[c] + center[i])
                gradient = taus[c] * result[i] - count[i] + intensity
                value = moment[c, i, pl.ds(row, 8), :] - kicks[c] * gradient
                moment[c, i, pl.ds(row, 8), :] = value
                target[c, i, pl.ds(row, 8), :] = center[i] + sizes[c] * value
                if carry and i < 2:
                    carry[c] += center[i] * result[i]
                    carry[2 + c] += intensity
        return carry and tuple(carry)

    return sweep(body, zeros(4), depth)


def advance_known(source, target, moment, counts, slope, growth, factor, tau, size, depth):
    factors = [splat(factor, c) for c in range(2)]
    taus = [splat(tau, c) for c in range(2)]
    sizes = [splat(size, c) for c in range(2)]

    def body(row, carry):
        here = pl.ds(row, 8)
        count = [counts[i, here, :] for i in range(3)]
        for c in range(2):
            for i in range(3):
                gradient = taus[c] * slope[c, i, here, :] - count[i]
                gradient += factors[c] * growth[c, i, here, :]
                value = moment[c, i, here, :] - sizes[c] * gradient
                moment[c, i, here, :] = value
                target[c, i, here, :] = source[c, i, here, :] + sizes[c] * value
        return carry

    loop(TOP - depth, END + depth, body, ())


def examine(field, kappa, slope, growth, lead, depth):
    lane = lanes()
    leads = [splat(lead, c) for c in range(2)]

    def body(row, carry):
        carry = carry and list(carry)
        for c in range(2):
            center, result = applied(field, kappa, c, row, lane, 3)
            for i in range(3):
                power = jnp.exp(leads[c] + center[i])
                slope[c, i, pl.ds(row, 8), :] = result[i]
                growth[c, i, pl.ds(row, 8), :] = power
                if carry and i < 2:
                    carry[c] += center[i] * result[i]
                    carry[2 + c] += power
        return carry and tuple(carry)

    return sweep(body, zeros(4), depth)


def put_sums(out, values):
    lane = lax.broadcasted_iota(jnp.int32, (1, 8), 1)
    row = jnp.zeros((1, 8), F32)
    for i, value in enumerate(values):
        total = jnp.sum(jnp.sum(value, axis=0, keepdims=True), axis=1, keepdims=True)
        row = jnp.where(lane == i, total, row)
    out[...] = jnp.broadcast_to(row[None], out.shape)


OFFSET, SCALE, SPEED_0, SPEED_1, STEP, COUNT = range(6)


def load_kernel(
    latent, momentum, counts_in, kappa_in, hyper, speed, size,
    state, left, right, low, table, raw, small, sems,
):
    field, moment, counts, kappa, _, _ = views(state)
    copies = [(hyper, small.at[pl.ds(0, 2)]), (speed, small.at[pl.ds(2, 2)])]
    copies.append((size, small.at[pl.ds(4, 1)]))
    for i in range(2):
        cols = pl.ds(128 * i, 128)
        own = pl.ds(TOP, SIZE)
        for c in range(2):
            copies.append((latent.at[c, :, cols], field.at[c, i, own, :]))
            copies.append((momentum.at[c, :, cols], moment.at[c, i, own, :]))
        copies.append((counts_in.at[:, cols], raw.at[i]))
        copies.append((kappa_in.at[:, cols], kappa.at[i, own, :]))
    copies = [pltpu.make_async_copy(a, b, sems.at[n]) for n, (a, b) in enumerate(copies)]
    for copy in copies:
        copy.start()
    for copy in copies:
        copy.wait()
    lane = lanes()
    group = lane // HALO

    def body(row, carry):
        here = pl.ds(pl.multiple_of(row - TOP, 8), 8)
        own = pl.ds(row, 8)
        for out, tile, base in ((left, 0, 0), (right, 1, HALO)):
            count = raw[tile, here, :].astype(F32)
            counts[tile, own, :] = count
            diagonal = kappa[tile, own, :] + 4.0
            kappa[tile, own, :] = diagonal
            parts = [
                field[0, tile, own, :],
                field[1, tile, own, :],
                moment[0, tile, own, :],
                moment[1, tile, own, :],
                count,
                diagonal,
            ]
            packed = jnp.zeros((8, 128), F32)
            for n, part in enumerate(parts):
                shift = (HALO * n + base) % 128
                moved = part if shift == 0 else pltpu.roll(part, shift, 1)
                packed = jnp.where(group == n, moved, packed)
            out[here, :] = packed
        return carry

    loop(TOP, END, body, ())
    for c in range(2):
        for i in range(2):
            low[pl.ds(c, 1), pl.ds(128 * i, 128)] = field[c, i, pl.ds(TOP, 1), :]
    table[...] = jnp.zeros((8, 128), F32)
    table[pl.ds(0, 5), pl.ds(0, 2)] = small[...]


def local_sums_kernel(table, state, partial):
    field, _, counts, kappa, _, _ = views(state)
    lane = lanes()
    offset = table[pl.ds(OFFSET, 1), pl.ds(0, 2)]
    offsets = [splat(offset, c) for c in range(2)]

    def body(row, carry):
        carry = list(carry)
        inside = lax.broadcasted_iota(jnp.int32, (8, 128), 0) + row < END - 1
        for i in range(2):
            carry[4] += counts[i, pl.ds(row, 8), :]
        for c in range(2):
            tiles = [field[c, i, pl.ds(row, 8), :] for i in range(2)]
            right0 = pltpu.roll(tiles[0], 127, 1)
            right1 = pltpu.roll(tiles[1], 127, 1)
            beside = [jnp.where(lane == 127, right1, right0), jnp.where(lane == 127, 0.0, right1)]
            for i in range(2):
                below = jnp.where(inside, field[c, i, pl.ds(row + 1, 8), :], 0.0)
                weight = kappa[i, pl.ds(row, 8), :] * tiles[i]
                carry[c] += tiles[i] * (weight - 2.0 * (beside[i] + below))
                carry[2 + c] += jnp.exp(offsets[c] + tiles[i])
        return tuple(carry)

    put_sums(partial, loop(TOP, END, body, zeros(5)))


def edges_kernel(state, from_right, below, partial, spread):
    field = views(state)[0]
    lane = lanes()

    def body(row, carry):
        carry = list(carry)
        buffer = from_right[pl.ds(pl.multiple_of(row - TOP, 8), 8), :]
        for c in range(2):
            other = buffer if c == 0 else pltpu.roll(buffer, 128 - HALO * c, 1)
            edge = pltpu.roll(field[c, 1, pl.ds(row, 8), :], 1, 1) * other
            carry[c] += jnp.where(lane == 0, edge, 0.0)
        return tuple(carry)

    edges = loop(TOP, END, body, zeros(2))
    index = lax.broadcasted_iota(jnp.int32, (1, 8), 1)
    row = partial[0]
    for c in range(2):
        total = jnp.sum(jnp.sum(edges[c], axis=0, keepdims=True), axis=1, keepdims=True)
        for i in range(2):
            own = field[c, i, pl.ds(END - 1, 1), :]
            other = below[pl.ds(c, 1), pl.ds(128 * i, 128)]
            total += jnp.sum(own * other, axis=1, keepdims=True)
        row -= jnp.where(index == c, 2.0 * total, 0.0)
    spread[...] = jnp.broadcast_to(row[None], spread.shape)


def unpack(buffers, lane, n):
    from_right, from_left = buffers
    near = HALO * n % 128
    far = (HALO * n + HALO) % 128
    a = from_right if near == 0 else pltpu.roll(from_right, 128 - near, 1)
    b = from_left if far == 0 else pltpu.roll(from_left, 128 - far, 1)
    return jnp.where(lane < HALO, a, jnp.where(lane >= 128 - HALO, b, 0.0))


def parts_of(state):
    field, moment, counts, kappa, _, _ = views(state)
    return [field.at[0], field.at[1], moment.at[0], moment.at[1], counts, kappa]


def columns_kernel(state_in, from_right, from_left, state, up, down):
    del state_in
    lane = lanes()
    parts = parts_of(state)

    def body(row, carry):
        here = pl.ds(pl.multiple_of(row - TOP, 8), 8)
        buffers = (from_right[here, :], from_left[here, :])
        for n, part in enumerate(parts):
            part[2, pl.ds(row, 8), :] = unpack(buffers, lane, n)
        return carry

    loop(TOP, END, body, ())
    for out, row, here in ((up, TOP, 0), (down, END - HALO, SIZE - HALO)):
        for n, part in enumerate(parts):
            for i in range(2):
                out[pl.ds(HALO * n, HALO), pl.ds(128 * i, 128)] = part[i, pl.ds(row, HALO), :]
        corner = pl.ds(HALO * FIELDS, HALO)
        out[corner, pl.ds(0, 128)] = from_right[pl.ds(here, HALO), :]
        out[corner, pl.ds(128, 128)] = from_left[pl.ds(here, HALO), :]


def unpack_rows(from_above, from_below, state):
    lane = lanes()
    parts = parts_of(state)
    for buffer, row in ((from_above, GUARD), (from_below, END)):
        for block in range(0, HALO, 8):
            corner = pl.ds(HALO * FIELDS + block, 8)
            buffers = (buffer[corner, pl.ds(0, 128)], buffer[corner, pl.ds(128, 128)])
            for n, part in enumerate(parts):
                for i in range(2):
                    part[i, pl.ds(row + block, 8), :] = buffer[
                        pl.ds(HALO * n + block, 8), pl.ds(128 * i, 128)
                    ]
                part[2, pl.ds(row + block, 8), :] = unpack(buffers, lane, n)


def sum_of(received):
    return jnp.sum(received[...], axis=0)


def read_table(table):
    return [table[pl.ds(i, 1), pl.ds(0, 2)] for i in range(6)]


def write_table(out, rows):
    out[...] = jnp.zeros((8, 128), F32)
    for i, row in enumerate(rows):
        out[pl.ds(i, 1), pl.ds(0, 2)] = row


def accel_of(quadratic, intensity, scale, count, total):
    return (intensity / total - count, 0.5 * jnp.exp(scale) * quadratic / total - 0.5)


def first_step_kernel(
    total, table, received, from_above, from_below, state_in, table_out, state, partial, other
):
    del state_in
    unpack_rows(from_above, from_below, state)
    field, moment, counts, kappa, slope, growth = views(state)
    reduced = sum_of(received)
    offset, scale, speed_0, speed_1, size, _ = read_table(table)
    quadratic, intensity = reduced[:, 0:2], reduced[:, 2:4]
    count = jnp.broadcast_to(reduced[:, 4:5], (1, 2)) / total
    a_0, a_1 = accel_of(quadratic, intensity, scale, count, total)
    advance(field, other, moment, counts, kappa, offset, jnp.exp(scale), size, 0.5, HALO)
    speed_0, speed_1 = speed_0 - 0.5 * size * a_0, speed_1 - 0.5 * size * a_1
    offset, scale = offset + size * speed_0, scale + size * speed_1
    near = advance(other, field, moment, counts, kappa, offset, jnp.exp(scale), size, 1.0, HALO)
    far = examine(field, kappa, slope, growth, offset - SHIFT, HALO // 2)
    put_sums(partial, (*near, *far))
    write_table(table_out, (offset, scale, speed_0, speed_1, size, count))


def two_params(table, received, total):
    reduced = sum_of(received)
    offset, scale, speed_0, speed_1, size, count = read_table(table)
    before = offset
    a_0, a_1 = accel_of(reduced[:, 0:2], reduced[:, 2:4], scale, count, total)
    speed_0, speed_1 = speed_0 - size * a_0, speed_1 - size * a_1
    offset, scale = offset + size * speed_0, scale + size * speed_1
    factor = jnp.exp(offset - before + SHIFT)
    intensity = reduced[:, 6:8] * factor
    a_0, a_1 = accel_of(reduced[:, 4:6], intensity, scale, count, total)
    return offset, scale, speed_0, speed_1, size, count, a_0, a_1, factor


def two_steps_kernel(total, table, received, state_in, table_out, state, partial, other):
    del state_in
    field, moment, counts, kappa, slope, growth = views(state)
    offset, scale, speed_0, speed_1, size, count, a_0, a_1, factor = two_params(table, received, total)
    advance_known(
        field, other, moment, counts, slope, growth, factor, jnp.exp(scale), size, HALO // 2
    )
    speed_0, speed_1 = speed_0 - size * a_0, speed_1 - size * a_1
    offset, scale = offset + size * speed_0, scale + size * speed_1
    near = advance(other, field, moment, counts, kappa, offset, jnp.exp(scale), size, 1.0, HALO // 2)
    far = examine(field, kappa, slope, growth, offset - SHIFT, HALO // 2)
    put_sums(partial, (*near, *far))
    write_table(table_out, (offset, scale, speed_0, speed_1, size, count))


def last_kernel(
    total, table, received, state,
    latent_out, momentum_out, hyper_out, velocity_out, result, sems,
):
    field, moment, counts, _, slope, growth = views(state)
    copies = []
    for c in range(2):
        for i in range(2):
            cols = pl.ds(128 * i, 128)
            copies.append((field.at[c, i, pl.ds(TOP, SIZE), :], latent_out.at[c, :, cols]))
    for c in range(2):
        for i in range(2):
            cols = pl.ds(128 * i, 128)
            copies.append((result.at[c, i], momentum_out.at[c, :, cols]))
    copies = [pltpu.make_async_copy(a, b, sems.at[n]) for n, (a, b) in enumerate(copies)]
    for copy in copies[:4]:
        copy.start()
    offset, scale, speed_0, speed_1, size, _, a_0, a_1, factor = two_params(table, received, total)
    tau = jnp.exp(scale)
    for c in range(2):
        tau_c, factor_c, half = splat(tau, c), splat(factor, c), 0.5 * splat(size, c)

        def body(row, carry, c=c, tau_c=tau_c, factor_c=factor_c, half=half):
            here = pl.ds(row, 8)
            out = pl.ds(pl.multiple_of(row - TOP, 8), 8)
            for i in range(2):
                gradient = tau_c * slope[c, i, here, :] - counts[i, here, :]
                gradient += factor_c * growth[c, i, here, :]
                result[c, i, out, :] = moment[c, i, here, :] - half * gradient
            return carry

        loop(TOP, END, body, ())
        for copy in copies[4 + 2 * c : 6 + 2 * c]:
            copy.start()
    hyper_out[pl.ds(0, 1), :] = offset
    hyper_out[pl.ds(1, 1), :] = scale
    velocity_out[pl.ds(0, 1), :] = speed_0 - 0.5 * size * a_0
    velocity_out[pl.ds(1, 1), :] = speed_1 - 0.5 * size * a_1
    for copy in copies:
        copy.wait()


def vmem(*shape):
    return pltpu.VMEM(shape, F32)


def held(array):
    return pltpu.with_memory_space_constraint(array, pltpu.VMEM)


STATE = vmem(10, 3, ROWS, 128)
PARAMS = pltpu.CompilerParams(vmem_limit_bytes=8 << 20)


def ring(x, axes, step):
    count = lax.axis_size(axes)
    return lax.ppermute(x, axes, [(i, (i + step) % count) for i in range(count)])


def exchange(spread):
    return lax.all_to_all(spread, ALL, 0, 0, tiled=True)


def shards(latent, momentum, hyper_params, velocity, step_size, counts, kappa_field):
    devices = lax.axis_size(ALL)
    total = float(latent.shape[1] * latent.shape[2] * devices)
    spread = vmem(devices, 1, 8)
    small_table = jax.ShapeDtypeStruct((8, 128), F32)
    given = (latent, momentum, counts, kappa_field, hyper_params, velocity, step_size[None])
    state, left, right, low, table = pl.pallas_call(
        load_kernel,
        out_shape=(STATE, vmem(SIZE, 128), vmem(SIZE, 128), vmem(2, SIZE), vmem(8, 128)),
        in_specs=[ANY] * 7,
        out_specs=(VMEM,) * 5,
        scratch_shapes=[
            pltpu.VMEM((2, SIZE, 128), jnp.int32),
            vmem(5, 2),
            pltpu.SemaphoreType.DMA((15,)),
        ],
        compiler_params=PARAMS,
        name="load",
    )(*(pltpu.with_memory_space_constraint(a, pltpu.HBM) for a in given))
    from_right, from_left = ring(left, COL, -1), ring(right, COL, 1)
    below = ring(low, ROW, -1)
    partial = pl.pallas_call(
        local_sums_kernel,
        out_shape=vmem(1, 1, 8),
        in_specs=[VMEM] * 2,
        out_specs=VMEM,
        compiler_params=PARAMS,
        name="local_sums",
    )(held(table), held(state))
    partial = pl.pallas_call(
        edges_kernel,
        out_shape=spread,
        in_specs=[VMEM] * 4,
        out_specs=VMEM,
        compiler_params=PARAMS,
        name="edges",
    )(held(state), from_right, below, partial)
    edge = vmem(HALO * (FIELDS + 1), SIZE)
    state, up, down = pl.pallas_call(
        columns_kernel,
        out_shape=(STATE, edge, edge),
        in_specs=[VMEM] * 3,
        out_specs=(VMEM,) * 3,
        input_output_aliases={0: 0},
        compiler_params=PARAMS,
        name="columns",
    )(held(state), from_right, from_left)
    from_below, from_above = ring(up, ROW, -1), ring(down, ROW, 1)
    received = exchange(partial)
    table, state, partial = pl.pallas_call(
        functools.partial(first_step_kernel, total),
        out_shape=(small_table, STATE, spread),
        in_specs=[VMEM] * 5,
        out_specs=(VMEM,) * 3,
        input_output_aliases={4: 1},
        scratch_shapes=[vmem(2, 3, ROWS, 128)],
        compiler_params=PARAMS,
        name="first_steps",
    )(table, received, from_above, from_below, held(state))
    for _ in range(STEPS // 2 - 1):
        received = exchange(partial)
        table, state, partial = pl.pallas_call(
            functools.partial(two_steps_kernel, total),
            out_shape=(small_table, STATE, spread),
            in_specs=[VMEM] * 3,
            out_specs=(VMEM,) * 3,
            input_output_aliases={2: 1},
            scratch_shapes=[vmem(2, 3, ROWS, 128)],
            compiler_params=PARAMS,
            name="two_steps",
        )(table, received, held(state))
    received = exchange(partial)
    return pl.pallas_call(
        functools.partial(last_kernel, total),
        out_shape=(
            jax.ShapeDtypeStruct(latent.shape, F32),
            jax.ShapeDtypeStruct(latent.shape, F32),
            jax.ShapeDtypeStruct((2, 2), F32),
            jax.ShapeDtypeStruct((2, 2), F32),
        ),
        in_specs=[VMEM] * 3,
        out_specs=(ANY, ANY, VMEM, VMEM),
        scratch_shapes=[vmem(2, 2, SIZE, 128), pltpu.SemaphoreType.DMA((8,))],
        compiler_params=PARAMS,
        name="last",
    )(table, received, held(state))


def solution(mesh):
    torus = Mesh(mesh.devices.reshape(2, 4, 2, 4, 2), ALL)
    return jax.shard_map(
        shards,
        mesh=torus,
        in_specs=(P(None, ROW, COL), P(None, ROW, COL), P(), P(), P(), P(ROW, COL), P(ROW, COL)),
        out_specs=(P(None, ROW, COL), P(None, ROW, COL), P(), P()),
        check_vma=False,
    )
```

time: 145 us -> 119 us (0.82)
  Pallas kernels: 36.3 us -> 17.7 us
  blocking collectives: 68.7 us -> 85.4 us
  waiting for transfers between devices: 9.86 us -> 0.28 us
  starting transfers between devices: 21.5 us -> 14.5 us
  local copies, waits for them, and re-layouts: 6.2 us -> 0 us
    all_to_all x5 -> x6, blocking collectives: 68.7 us -> 85.4 us  [exchange(): return lax.all_to_all(spread, ALL, 0, 0, tiled=True)]
    pallas_call x4, Pallas kernels: 22.7 us -> 8.86 us  [shards(): pl.pallas_call(functools.partial(two_steps_kernel, total), out_shape=(sma...]
    all_to_all x1 -> x0, waiting for transfers between devices: 9.12 us -> none  [all_sum(): return jnp.sum(lax.all_to_all(spread, ALL, 0, 0, tiled=True), axis=0)]
    all_to_all x1 -> x0, starting transfers between devices: 7.01 us -> none  [all_sum(): return jnp.sum(lax.all_to_all(spread, ALL, 0, 0, tiled=True), axis=0)]
    unnamed x15 -> x0, local copies, waits for them, and re-layouts: 4.65 us -> none
    pallas_call x1, Pallas kernels: 4.48 us -> 1.82 us  [shards(): pl.pallas_call(functools.partial(last_kernel, total), out_shape=(jax.Shap...]
    pallas_call x1, Pallas kernels: 5.58 us -> 3.6 us  [shards(): pl.pallas_call(functools.partial(first_step_kernel, total), out_shape=(sm...]
    pallas_call x2 -> x4, Pallas kernels: 3.58 us -> 3.47 us  [the longest x1 2.12 us: shards(): pl.pallas_call(load_kernel, out_shape=(STATE, vmem(SIZE, 128), vmem(SIZE,...]
  transfers between devices with their start and end apart: 6 -> 5, of which waited for: 2 -> 1; matrix products, arithmetic and copies ran while one was open for 1% -> 0% of each run, Pallas kernels for 0% -> 1%
where the time goes in v2:
time: 119 us
  blocking collectives  85.4 us (72%)
  Pallas kernels  17.7 us (15%)
  starting transfers between devices  14.5 us (12%)
    all_to_all x6, blocking collectives, exchange(): return lax.all_to_all(spread, ALL, 0, 0, tiled=True)  85.4 us
    ppermute x5, starting transfers between devices, ring(): lax.ppermute(x, axes, [(i, (i + step) % count) for i in range(count)])  14.5 us
    pallas_call x4, Pallas kernels, shards(): pl.pallas_call(functools.partial(two_steps_kernel, total), out_shape=(sma...  8.86 us
    pallas_call x1, Pallas kernels, shards(): pl.pallas_call(functools.partial(first_step_kernel, total), out_shape=(sm...  3.6 us
  transfers between devices with their start and end apart: 5, of which 1 were waited for; matrix products, arithmetic and copies ran while one was open for 0% of the time, Pallas kernels for 1%

profile of v2, /device:TPU:1, one launch (start us, length us, event | category | flops | bytes accessed | tf_op | source)
XLA Modules:
  0.0 118.6 jit_solution(12035192148373846776)
XLA Ops:
  0.6 2.1 %load.1 = (f32[10,3,304,128]{3,2,1,0:T(8,128)S(1)}, f32[256,128]{1,0:T(8,128)S(1)}, f32[256,128]{1,0:T(8,128)S(1)}, f32[2,256]{1,0:T(2,128)S(1)}, f32[8,128]{1,0:T(8,128)S(1)}) custom-call(f32[2,256,256]{2,1,0:T(8,128)} %latent.1, f32[2,256,256]{2,1,0:T(8,128)} %momentum.1, s32[256,256]{1,0:T(8,128)} %counts_in.1, f32[256,256]{1,0:T(8,128)} %kappa_in.1, ...), custom_call_target="tpu_custom_call" | custom-call | tf_op jit(solution)/shard_map/load/pallas_call | solution.py:453
  2.8 1.5 %collective-permute-start = (f32[256,128]{1,0:T(8,128)S(1)}, f32[256,128]{1,0:T(8,128)S(1)}, u32[]{:S(2)}, u32[]{:S(2)}) collective-permute-start(f32[256,128]{1,0:T(8,128)S(1)} %get-tuple-element.29), channel_id=1, source_target_pairs={{0,15},{1,0},{2,1},{3,2},{4,3},{5,4},{6,5},{7,6},{8,7},{9,8},{10,9... | collective-permute-start | bytes 393224 | tf_op jit(solution)/shard_map/ppermute | solution.py:440
  4.3 1.3 %collective-permute-start.2 = (f32[256,128]{1,0:T(8,128)S(1)}, f32[256,128]{1,0:T(8,128)S(1)}, u32[]{:S(2)}, u32[]{:S(2)}) collective-permute-start(f32[256,128]{1,0:T(8,128)S(1)} %get-tuple-element.31), channel_id=1, source_target_pairs={{0,1},{1,2},{2,3},{3,4},{4,5},{5,6},{6,7},{7,8},{8,9},{9,10},{10,1... | collective-permute-start | bytes 393224 | tf_op jit(solution)/shard_map/ppermute | solution.py:440
  5.6 6.2 %collective-permute-start.1 = (f32[2,256]{1,0:T(2,128)S(1)}, f32[2,256]{1,0:T(2,128)S(1)}, u32[]{:S(2)}, u32[]{:S(2)}) collective-permute-start(f32[2,256]{1,0:T(2,128)S(1)} %get-tuple-element.30), channel_id=1, source_target_pairs={{0,112},{16,0},{32,16},{48,32},{64,48},{80,64},{96,80},{112,96},{1... | collective-permute-start | bytes 6152 | tf_op jit(solution)/shard_map/ppermute | solution.py:440
  11.8 0.5 local_sums.1.partial
  12.3 0.3 collective-permute-done.1.below
  12.6 0.0 collective-permute-done.from_right
  12.6 0.4 edges.1
  12.9 0.0 collective-permute-done.2.from_left
  12.9 0.5 columns.1
  13.5 0.1 collective-permute-start.3
  13.5 5.4 %collective-permute-start.4 = (f32[112,256]{1,0:T(8,128)S(1)}, f32[112,256]{1,0:T(8,128)S(1)}, u32[]{:S(2)}, u32[]{:S(2)}) collective-permute-start(f32[112,256]{1,0:T(8,128)S(1)} %get-tuple-element.33), channel_id=1, source_target_pairs={{0,112},{16,0},{32,16},{48,32},{64,48},{80,64},{96,80},{112,96},{1... | collective-permute-start | bytes 344072 | tf_op jit(solution)/shard_map/ppermute | solution.py:440
  18.9 16.7 %all_to_all.30.received = f32[128,1,8]{2,1,0:T(1,128)S(1)} all-to-all(f32[128,1,8]{2,1,0:T(1,128)S(1)} %edges.1), channel_id=1, replica_groups=mesh['row_0'=2,'row_1'=4,'col_0'=2,'col_1'=4,'col_2'=2] {'row_0','row_1'..., dimensions={0} | all-to-all | bytes 8192 | tf_op jit(solution)/shard_map/all_to_all | solution.py:444
  35.6 0.0 collective-permute-done.3.from_above
  35.6 0.0 collective-permute-done.4.from_below
  35.6 3.6 %first_steps.1 = (f32[8,128]{1,0:T(8,128)S(1)}, f32[10,3,304,128]{3,2,1,0:T(8,128)S(1)}, f32[128,1,8]{2,1,0:T(1,128)S(1)}) custom-call(f32[8,128]{1,0:T(8,128)S(1)} %get-tuple-element.27.table, f32[128,1,8]{2,1,0:T(1,128)S(1)} %all_to_all.30.received, f32[112,256]{1,0:T(8,128)S(1)} %collective-permute-done.3.from_above, ...), custom_call_target="tpu_custom_call", output_to_operand_aliasing={{1}: (4, {})} | custom-call | tf_op jit(solution)/shard_map/first_steps/pallas_call | solution.py:496
  39.2 13.7 %all_to_all.31.received = f32[128,1,8]{2,1,0:T(1,128)S(1)} all-to-all(f32[128,1,8]{2,1,0:T(1,128)S(1)} %get-tuple-element.36), channel_id=1, replica_groups=mesh['row_0'=2,'row_1'=4,'col_0'=2,'col_1'=4,'col_2'=2] {'row_0','row_1'..., dimensions={0} | all-to-all | bytes 8192 | tf_op jit(solution)/shard_map/all_to_all | solution.py:444
  53.0 2.2 %two_steps.4 = (f32[8,128]{1,0:T(8,128)S(1)}, f32[10,3,304,128]{3,2,1,0:T(8,128)S(1)}, f32[128,1,8]{2,1,0:T(1,128)S(1)}) custom-call(f32[8,128]{1,0:T(8,128)S(1)} %get-tuple-element.35.table, f32[128,1,8]{2,1,0:T(1,128)S(1)} %all_to_all.31.received, f32[10,3,304,128]{3,2,1,0:T(8,128)S(1)} %get-tuple-element.37.state_in), custom_call_target="tpu_custom_call", output_to_operand_aliasing={{1}: (2, {})} | custom-call | tf_op jit(solution)/shard_map/two_steps/pallas_call | solution.py:508
  55.2 13.7 %all_to_all.32.received = f32[128,1,8]{2,1,0:T(1,128)S(1)} all-to-all(f32[128,1,8]{2,1,0:T(1,128)S(1)} %get-tuple-element.39), channel_id=1, replica_groups=mesh['row_0'=2,'row_1'=4,'col_0'=2,'col_1'=4,'col_2'=2] {'row_0','row_1'..., dimensions={0} | all-to-all | bytes 8192 | tf_op jit(solution)/shard_map/all_to_all | solution.py:444
  68.9 2.2 %two_steps.5 = (f32[8,128]{1,0:T(8,128)S(1)}, f32[10,3,304,128]{3,2,1,0:T(8,128)S(1)}, f32[128,1,8]{2,1,0:T(1,128)S(1)}) custom-call(f32[8,128]{1,0:T(8,128)S(1)} %get-tuple-element.38.table, f32[128,1,8]{2,1,0:T(1,128)S(1)} %all_to_all.32.received, f32[10,3,304,128]{3,2,1,0:T(8,128)S(1)} %get-tuple-element.40.state_in), custom_call_target="tpu_custom_call", output_to_operand_aliasing={{1}: (2, {})} | custom-call | tf_op jit(solution)/shard_map/two_steps/pallas_call | solution.py:508
  71.2 13.7 %all_to_all.33.received = f32[128,1,8]{2,1,0:T(1,128)S(1)} all-to-all(f32[128,1,8]{2,1,0:T(1,128)S(1)} %get-tuple-element.42), channel_id=1, replica_groups=mesh['row_0'=2,'row_1'=4,'col_0'=2,'col_1'=4,'col_2'=2] {'row_0','row_1'..., dimensions={0} | all-to-all | bytes 8192 | tf_op jit(solution)/shard_map/all_to_all | solution.py:444
  84.9 2.2 %two_steps.6 = (f32[8,128]{1,0:T(8,128)S(1)}, f32[10,3,304,128]{3,2,1,0:T(8,128)S(1)}, f32[128,1,8]{2,1,0:T(1,128)S(1)}) custom-call(f32[8,128]{1,0:T(8,128)S(1)} %get-tuple-element.41.table, f32[128,1,8]{2,1,0:T(1,128)S(1)} %all_to_all.33.received, f32[10,3,304,128]{3,2,1,0:T(8,128)S(1)} %get-tuple-element.43.state_in), custom_call_target="tpu_custom_call", output_to_operand_aliasing={{1}: (2, {})} | custom-call | tf_op jit(solution)/shard_map/two_steps/pallas_call | solution.py:508
  87.1 13.7 %all_to_all.34.received = f32[128,1,8]{2,1,0:T(1,128)S(1)} all-to-all(f32[128,1,8]{2,1,0:T(1,128)S(1)} %get-tuple-element.45), channel_id=1, replica_groups=mesh['row_0'=2,'row_1'=4,'col_0'=2,'col_1'=4,'col_2'=2] {'row_0','row_1'..., dimensions={0} | all-to-all | bytes 8192 | tf_op jit(solution)/shard_map/all_to_all | solution.py:444
  100.9 2.2 %two_steps.7 = (f32[8,128]{1,0:T(8,128)S(1)}, f32[10,3,304,128]{3,2,1,0:T(8,128)S(1)}, f32[128,1,8]{2,1,0:T(1,128)S(1)}) custom-call(f32[8,128]{1,0:T(8,128)S(1)} %get-tuple-element.44.table, f32[128,1,8]{2,1,0:T(1,128)S(1)} %all_to_all.34.received, f32[10,3,304,128]{3,2,1,0:T(8,128)S(1)} %get-tuple-element.46.state_in), custom_call_target="tpu_custom_call", output_to_operand_aliasing={{1}: (2, {})} | custom-call | tf_op jit(solution)/shard_map/two_steps/pallas_call | solution.py:508
  103.1 13.7 %all_to_all.35.received = f32[128,1,8]{2,1,0:T(1,128)S(1)} all-to-all(f32[128,1,8]{2,1,0:T(1,128)S(1)} %get-tuple-element.48), channel_id=1, replica_groups=mesh['row_0'=2,'row_1'=4,'col_0'=2,'col_1'=4,'col_2'=2] {'row_0','row_1'..., dimensions={0} | all-to-all | bytes 8192 | tf_op jit(solution)/shard_map/all_to_all | solution.py:444
  116.8 1.8 %last.1 = (f32[2,256,256]{2,1,0:T(8,128)}, f32[2,256,256]{2,1,0:T(8,128)}, f32[2,2]{1,0:T(2,128)}, f32[2,2]{1,0:T(2,128)}) custom-call(f32[8,128]{1,0:T(8,128)S(1)} %get-tuple-element.47.table, f32[128,1,8]{2,1,0:T(1,128)S(1)} %all_to_all.35.received, f32[10,3,304,128]{3,2,1,0:T(8,128)S(1)} %get-tuple-element.49.state), custom_call_target="tpu_custom_call" | custom-call | tf_op jit(solution)/shard_map/last/pallas_call | solution.py:519
Async XLA Ops:
  2.8 9.8 %collective-permute-start = (f32[256,128]{1,0:T(8,128)S(1)}, f32[256,128]{1,0:T(8,128)S(1)}, u32[]{:S(2)}, u32[]{:S(2)}) collective-permute-start(f32[256,128]{1,0:T(8,128)S(1)} %get-tuple-element.29), channel_id=1, source_target_pairs={{0,15},{1,0},{2,1},{3,2},{4,3},{5,4},{6,5},{7,6},{8,7},{9,8},{10,9... | collective-permute-start | bytes 393224 | tf_op jit(solution)/shard_map/ppermute | solution.py:440
  4.3 8.7 %collective-permute-start.2 = (f32[256,128]{1,0:T(8,128)S(1)}, f32[256,128]{1,0:T(8,128)S(1)}, u32[]{:S(2)}, u32[]{:S(2)}) collective-permute-start(f32[256,128]{1,0:T(8,128)S(1)} %get-tuple-element.31), channel_id=1, source_target_pairs={{0,1},{1,2},{2,3},{3,4},{4,5},{5,6},{6,7},{7,8},{8,9},{9,10},{10,1... | collective-permute-start | bytes 393224 | tf_op jit(solution)/shard_map/ppermute | solution.py:440
  5.6 7.0 %collective-permute-start.1 = (f32[2,256]{1,0:T(2,128)S(1)}, f32[2,256]{1,0:T(2,128)S(1)}, u32[]{:S(2)}, u32[]{:S(2)}) collective-permute-start(f32[2,256]{1,0:T(2,128)S(1)} %get-tuple-element.30), channel_id=1, source_target_pairs={{0,112},{16,0},{32,16},{48,32},{64,48},{80,64},{96,80},{112,96},{1... | collective-permute-start | bytes 6152 | tf_op jit(solution)/shard_map/ppermute | solution.py:440
  13.5 22.2 %collective-permute-start.3 = (f32[112,256]{1,0:T(8,128)S(1)}, f32[112,256]{1,0:T(8,128)S(1)}, u32[]{:S(2)}, u32[]{:S(2)}) collective-permute-start(f32[112,256]{1,0:T(8,128)S(1)} %get-tuple-element.32), channel_id=1, source_target_pairs={{0,16},{16,32},{32,48},{48,64},{64,80},{80,96},{96,112},{112,0},{1... | collective-permute-start | bytes 344072 | tf_op jit(solution)/shard_map/ppermute | solution.py:440
  13.5 22.1 %collective-permute-start.4 = (f32[112,256]{1,0:T(8,128)S(1)}, f32[112,256]{1,0:T(8,128)S(1)}, u32[]{:S(2)}, u32[]{:S(2)}) collective-permute-start(f32[112,256]{1,0:T(8,128)S(1)} %get-tuple-element.33), channel_id=1, source_target_pairs={{0,112},{16,0},{32,16},{48,32},{64,48},{80,64},{96,80},{112,96},{1... | collective-permute-start | bytes 344072 | tf_op jit(solution)/shard_map/ppermute | solution.py:440

commit v3 on v2

--- a/solution.py
+++ b/solution.py
@@ -20,11 +20,11 @@
 ROWS = 2 * TOP + SIZE
 END = TOP + SIZE
 FIELDS = 6
+PIECES = 4
 SHIFT = 8.0
 VMEM = pl.BlockSpec(memory_space=pltpu.VMEM)
 ANY = pl.BlockSpec(memory_space=pl.ANY)
 F32 = jnp.float32
-UNROLL = 16
 
 
 def views(state):
@@ -63,10 +63,9 @@
 
 
 def loop(start, stop, body, init):
-    def step(i, carry):
-        return body(pl.multiple_of(start + 8 * i, 8), carry)
-
-    return lax.fori_loop(0, (stop - start) // 8, step, init, unroll=UNROLL)
+    for row in range(start, stop, 8):
+        init = body(row, init)
+    return init
 
 
 def sweep(body, carry, depth):
@@ -181,7 +180,7 @@
     group = lane // HALO
 
     def body(row, carry):
-        here = pl.ds(pl.multiple_of(row - TOP, 8), 8)
+        here = pl.ds(row - TOP, 8)
         own = pl.ds(row, 8)
         for out, tile, base in ((left, 0, 0), (right, 1, HALO)):
             count = raw[tile, here, :].astype(F32)
@@ -244,7 +243,7 @@
 
     def body(row, carry):
         carry = list(carry)
-        buffer = from_right[pl.ds(pl.multiple_of(row - TOP, 8), 8), :]
+        buffer = from_right[pl.ds(row - TOP, 8), :]
         for c in range(2):
             other = buffer if c == 0 else pltpu.roll(buffer, 128 - HALO * c, 1)
             edge = pltpu.roll(field[c, 1, pl.ds(row, 8), :], 1, 1) * other
@@ -284,7 +283,7 @@
     parts = parts_of(state)
 
     def body(row, carry):
-        here = pl.ds(pl.multiple_of(row - TOP, 8), 8)
+        here = pl.ds(row - TOP, 8)
         buffers = (from_right[here, :], from_left[here, :])
         for n, part in enumerate(parts):
             part[2, pl.ds(row, 8), :] = unpack(buffers, lane, n)
@@ -366,8 +365,21 @@
     return offset, scale, speed_0, speed_1, size, count, a_0, a_1, factor
 
 
-def two_steps_kernel(total, table, received, state_in, table_out, state, partial, other):
+def field_copies(field, out, sems):
+    pairs = [(c, i) for c in range(2) for i in range(2)]
+    return [
+        pltpu.make_async_copy(
+            field.at[c, i, pl.ds(TOP, SIZE), :], out.at[c, :, pl.ds(128 * i, 128)], sems.at[n]
+        )
+        for n, (c, i) in enumerate(pairs)
+    ]
+
+
+def two_steps_kernel(
+    total, final, table, received, state_in, table_out, state, partial, *more
+):
     del state_in
+    *latent_out, other = more[: 1 + final]
     field, moment, counts, kappa, slope, growth = views(state)
     offset, scale, speed_0, speed_1, size, count, a_0, a_1, factor = two_params(table, received, total)
     advance_known(
@@ -376,49 +388,56 @@
     speed_0, speed_1 = speed_0 - size * a_0, speed_1 - size * a_1
     offset, scale = offset + size * speed_0, scale + size * speed_1
     near = advance(other, field, moment, counts, kappa, offset, jnp.exp(scale), size, 1.0, HALO // 2)
+    copies = []
+    if final:
+        copies = field_copies(field, latent_out[0], more[-1])
+        for copy in copies:
+            copy.start()
     far = examine(field, kappa, slope, growth, offset - SHIFT, HALO // 2)
     put_sums(partial, (*near, *far))
     write_table(table_out, (offset, scale, speed_0, speed_1, size, count))
+    for copy in copies:
+        copy.wait()
 
 
 def last_kernel(
-    total, table, received, state,
-    latent_out, momentum_out, hyper_out, velocity_out, result, sems,
+    total, table, received, state, momentum_out, hyper_out, velocity_out, result, small, sems
 ):
-    field, moment, counts, _, slope, growth = views(state)
-    copies = []
-    for c in range(2):
-        for i in range(2):
-            cols = pl.ds(128 * i, 128)
-            copies.append((field.at[c, i, pl.ds(TOP, SIZE), :], latent_out.at[c, :, cols]))
-    for c in range(2):
-        for i in range(2):
-            cols = pl.ds(128 * i, 128)
-            copies.append((result.at[c, i], momentum_out.at[c, :, cols]))
-    copies = [pltpu.make_async_copy(a, b, sems.at[n]) for n, (a, b) in enumerate(copies)]
-    for copy in copies[:4]:
-        copy.start()
+    _, moment, counts, _, slope, growth = views(state)
     offset, scale, speed_0, speed_1, size, _, a_0, a_1, factor = two_params(table, received, total)
     tau = jnp.exp(scale)
-    for c in range(2):
-        tau_c, factor_c, half = splat(tau, c), splat(factor, c), 0.5 * splat(size, c)
-
-        def body(row, carry, c=c, tau_c=tau_c, factor_c=factor_c, half=half):
+    taus = [splat(tau, c) for c in range(2)]
+    factors = [splat(factor, c) for c in range(2)]
+    halves = [0.5 * splat(size, c) for c in range(2)]
+    for i, row in enumerate(
+        (offset, scale, speed_0 - 0.5 * size * a_0, speed_1 - 0.5 * size * a_1)
+    ):
+        small[i // 2, pl.ds(i % 2, 1), :] = row
+    copies = [
+        pltpu.make_async_copy(small.at[0], hyper_out, sems.at[2 * PIECES]),
+        pltpu.make_async_copy(small.at[1], velocity_out, sems.at[2 * PIECES + 1]),
+    ]
+    for copy in copies:
+        copy.start()
+    for n in range(PIECES):
+        start = n * SIZE // PIECES
+        rows = pl.ds(start, SIZE // PIECES)
+        for row in range(TOP + start, TOP + start + SIZE // PIECES, 8):
             here = pl.ds(row, 8)
-            out = pl.ds(pl.multiple_of(row - TOP, 8), 8)
             for i in range(2):
-                gradient = tau_c * slope[c, i, here, :] - counts[i, here, :]
-                gradient += factor_c * growth[c, i, here, :]
-                result[c, i, out, :] = moment[c, i, here, :] - half * gradient
-            return carry
-
-        loop(TOP, END, body, ())
-        for copy in copies[4 + 2 * c : 6 + 2 * c]:
-            copy.start()
-    hyper_out[pl.ds(0, 1), :] = offset
-    hyper_out[pl.ds(1, 1), :] = scale
-    velocity_out[pl.ds(0, 1), :] = speed_0 - 0.5 * size * a_0
-    velocity_out[pl.ds(1, 1), :] = speed_1 - 0.5 * size * a_1
+                count = counts[i, here, :]
+                for c in range(2):
+                    gradient = taus[c] * slope[c, i, here, :] - count
+                    gradient += factors[c] * growth[c, i, here, :]
+                    value = moment[c, i, here, :] - halves[c] * gradient
+                    result[c, pl.ds(row - TOP, 8), pl.ds(128 * i, 128)] = value
+        for c in range(2):
+            copies.append(
+                pltpu.make_async_copy(
+                    result.at[c, rows, :], momentum_out.at[c, rows, :], sems.at[2 * n + c]
+                )
+            )
+            copies[-1].start()
     for copy in copies:
         copy.wait()
 
@@ -503,33 +522,40 @@
         compiler_params=PARAMS,
         name="first_steps",
     )(table, received, from_above, from_below, held(state))
-    for _ in range(STEPS // 2 - 1):
+    latent_out = ()
+    result = jax.ShapeDtypeStruct(latent.shape, F32)
+    for index in range(STEPS // 2 - 1):
         received = exchange(partial)
-        table, state, partial = pl.pallas_call(
-            functools.partial(two_steps_kernel, total),
-            out_shape=(small_table, STATE, spread),
+        final = index == STEPS // 2 - 2
+        table, state, partial, *latent_out = pl.pallas_call(
+            functools.partial(two_steps_kernel, total, final),
+            out_shape=(small_table, STATE, spread) + final * (result,),
             in_specs=[VMEM] * 3,
-            out_specs=(VMEM,) * 3,
+            out_specs=(VMEM,) * 3 + final * (ANY,),
             input_output_aliases={2: 1},
-            scratch_shapes=[vmem(2, 3, ROWS, 128)],
+            scratch_shapes=[vmem(2, 3, ROWS, 128)] + final * [pltpu.SemaphoreType.DMA((4,))],
             compiler_params=PARAMS,
             name="two_steps",
         )(table, received, held(state))
     received = exchange(partial)
-    return pl.pallas_call(
+    momentum_out, hyper_out, velocity_out = pl.pallas_call(
         functools.partial(last_kernel, total),
         out_shape=(
-            jax.ShapeDtypeStruct(latent.shape, F32),
-            jax.ShapeDtypeStruct(latent.shape, F32),
+            result,
             jax.ShapeDtypeStruct((2, 2), F32),
             jax.ShapeDtypeStruct((2, 2), F32),
         ),
         in_specs=[VMEM] * 3,
-        out_specs=(ANY, ANY, VMEM, VMEM),
-        scratch_shapes=[vmem(2, 2, SIZE, 128), pltpu.SemaphoreType.DMA((8,))],
+        out_specs=(ANY,) * 3,
+        scratch_shapes=[
+            vmem(*latent.shape),
+            vmem(2, 2, 2),
+            pltpu.SemaphoreType.DMA((2 * PIECES + 2,)),
+        ],
         compiler_params=PARAMS,
         name="last",
     )(table, received, held(state))
+    return latent_out[0], momentum_out, hyper_out, velocity_out
 
 
 def solution(mesh):

time: 119 us -> 115 us (0.966)
  Pallas kernels: 17.7 us -> 13.9 us
    pallas_call x5, Pallas kernels: 10.7 us -> 8.87 us  [the longest x4 7.59 us: shards(): pl.pallas_call(functools.partial(two_steps_kernel, total, final), out_sha...]
    pallas_call x1, Pallas kernels: 3.6 us -> 1.86 us  [shards(): pl.pallas_call(functools.partial(first_step_kernel, total), out_shape=(sm...]
where the time goes in v3:
time: 115 us
  blocking collectives  85.4 us (74%)
  starting transfers between devices  14.5 us (13%)
  Pallas kernels  13.9 us (12%)
    all_to_all x6, blocking collectives, exchange(): return lax.all_to_all(spread, ALL, 0, 0, tiled=True)  85.4 us
    ppermute x5, starting transfers between devices, ring(): lax.ppermute(x, axes, [(i, (i + step) % count) for i in range(count)])  14.5 us
    pallas_call x4, Pallas kernels, shards(): pl.pallas_call(functools.partial(two_steps_kernel, total, final), out_sha...  7.59 us
  transfers between devices with their start and end apart: 5, of which 1 were waited for; matrix products, arithmetic and copies ran while one was open for 0% of the time, Pallas kernels for 1%

profile of v3, /device:TPU:1, one launch (start us, length us, event | category | flops | bytes accessed | tf_op | source)
XLA Modules:
  0.0 115.0 jit_solution(7701792980711370176)
XLA Ops:
  0.6 2.0 %load.1 = (f32[10,3,304,128]{3,2,1,0:T(8,128)S(1)}, f32[256,128]{1,0:T(8,128)S(1)}, f32[256,128]{1,0:T(8,128)S(1)}, f32[2,256]{1,0:T(2,128)S(1)}, f32[8,128]{1,0:T(8,128)S(1)}) custom-call(f32[2,256,256]{2,1,0:T(8,128)} %latent.1, f32[2,256,256]{2,1,0:T(8,128)} %momentum.1, s32[256,256]{1,0:T(8,128)} %counts_in.1, f32[256,256]{1,0:T(8,128)} %kappa_in.1, ...), custom_call_target="tpu_custom_call" | custom-call | tf_op jit(solution)/shard_map/load/pallas_call | solution.py:472
  2.7 1.5 %collective-permute-start = (f32[256,128]{1,0:T(8,128)S(1)}, f32[256,128]{1,0:T(8,128)S(1)}, u32[]{:S(2)}, u32[]{:S(2)}) collective-permute-start(f32[256,128]{1,0:T(8,128)S(1)} %get-tuple-element.33), channel_id=1, source_target_pairs={{0,15},{1,0},{2,1},{3,2},{4,3},{5,4},{6,5},{7,6},{8,7},{9,8},{10,9... | collective-permute-start | bytes 393224 | tf_op jit(solution)/shard_map/ppermute | solution.py:459
  4.2 1.3 %collective-permute-start.2 = (f32[256,128]{1,0:T(8,128)S(1)}, f32[256,128]{1,0:T(8,128)S(1)}, u32[]{:S(2)}, u32[]{:S(2)}) collective-permute-start(f32[256,128]{1,0:T(8,128)S(1)} %get-tuple-element.35), channel_id=1, source_target_pairs={{0,1},{1,2},{2,3},{3,4},{4,5},{5,6},{6,7},{7,8},{8,9},{9,10},{10,1... | collective-permute-start | bytes 393224 | tf_op jit(solution)/shard_map/ppermute | solution.py:459
  5.5 6.2 %collective-permute-start.1 = (f32[2,256]{1,0:T(2,128)S(1)}, f32[2,256]{1,0:T(2,128)S(1)}, u32[]{:S(2)}, u32[]{:S(2)}) collective-permute-start(f32[2,256]{1,0:T(2,128)S(1)} %get-tuple-element.34), channel_id=1, source_target_pairs={{0,112},{16,0},{32,16},{48,32},{64,48},{80,64},{96,80},{112,96},{1... | collective-permute-start | bytes 6152 | tf_op jit(solution)/shard_map/ppermute | solution.py:459
  11.7 0.4 local_sums.1.partial
  12.1 0.3 collective-permute-done.1.below
  12.5 0.0 collective-permute-done.from_right
  12.5 0.3 edges.1
  12.8 0.0 collective-permute-done.2.from_left
  12.8 0.4 columns.1
  13.2 0.1 collective-permute-start.3
  13.3 5.4 %collective-permute-start.4 = (f32[112,256]{1,0:T(8,128)S(1)}, f32[112,256]{1,0:T(8,128)S(1)}, u32[]{:S(2)}, u32[]{:S(2)}) collective-permute-start(f32[112,256]{1,0:T(8,128)S(1)} %get-tuple-element.37), channel_id=1, source_target_pairs={{0,112},{16,0},{32,16},{48,32},{64,48},{80,64},{96,80},{112,96},{1... | collective-permute-start | bytes 344072 | tf_op jit(solution)/shard_map/ppermute | solution.py:459
  18.7 16.7 %all_to_all.30.received = f32[128,1,8]{2,1,0:T(1,128)S(1)} all-to-all(f32[128,1,8]{2,1,0:T(1,128)S(1)} %edges.1), channel_id=1, replica_groups=mesh['row_0'=2,'row_1'=4,'col_0'=2,'col_1'=4,'col_2'=2] {'row_0','row_1'..., dimensions={0} | all-to-all | bytes 8192 | tf_op jit(solution)/shard_map/all_to_all | solution.py:463
  35.4 0.0 collective-permute-done.3.from_above
  35.4 0.0 collective-permute-done.4.from_below
  35.4 1.9 %first_steps.1 = (f32[8,128]{1,0:T(8,128)S(1)}, f32[10,3,304,128]{3,2,1,0:T(8,128)S(1)}, f32[128,1,8]{2,1,0:T(1,128)S(1)}) custom-call(f32[8,128]{1,0:T(8,128)S(1)} %get-tuple-element.31.table, f32[128,1,8]{2,1,0:T(1,128)S(1)} %all_to_all.30.received, f32[112,256]{1,0:T(8,128)S(1)} %collective-permute-done.3.from_above, ...), custom_call_target="tpu_custom_call", output_to_operand_aliasing={{1}: (4, {})} | custom-call | tf_op jit(solution)/shard_map/first_steps/pallas_call | solution.py:515
  37.3 13.7 %all_to_all.31.received = f32[128,1,8]{2,1,0:T(1,128)S(1)} all-to-all(f32[128,1,8]{2,1,0:T(1,128)S(1)} %get-tuple-element.40), channel_id=1, replica_groups=mesh['row_0'=2,'row_1'=4,'col_0'=2,'col_1'=4,'col_2'=2] {'row_0','row_1'..., dimensions={0} | all-to-all | bytes 8192 | tf_op jit(solution)/shard_map/all_to_all | solution.py:463
  51.0 1.8 %two_steps.4 = (f32[8,128]{1,0:T(8,128)S(1)}, f32[10,3,304,128]{3,2,1,0:T(8,128)S(1)}, f32[128,1,8]{2,1,0:T(1,128)S(1)}) custom-call(f32[8,128]{1,0:T(8,128)S(1)} %get-tuple-element.39.table, f32[128,1,8]{2,1,0:T(1,128)S(1)} %all_to_all.31.received, f32[10,3,304,128]{3,2,1,0:T(8,128)S(1)} %get-tuple-element.41.state_in), custom_call_target="tpu_custom_call", output_to_operand_aliasing={{1}: (2, {})} | custom-call | tf_op jit(solution)/shard_map/two_steps/pallas_call | solution.py:530
  52.8 13.7 %all_to_all.32.received = f32[128,1,8]{2,1,0:T(1,128)S(1)} all-to-all(f32[128,1,8]{2,1,0:T(1,128)S(1)} %get-tuple-element.43), channel_id=1, replica_groups=mesh['row_0'=2,'row_1'=4,'col_0'=2,'col_1'=4,'col_2'=2] {'row_0','row_1'..., dimensions={0} | all-to-all | bytes 8192 | tf_op jit(solution)/shard_map/all_to_all | solution.py:463
  66.5 1.8 %two_steps.5 = (f32[8,128]{1,0:T(8,128)S(1)}, f32[10,3,304,128]{3,2,1,0:T(8,128)S(1)}, f32[128,1,8]{2,1,0:T(1,128)S(1)}) custom-call(f32[8,128]{1,0:T(8,128)S(1)} %get-tuple-element.42.table, f32[128,1,8]{2,1,0:T(1,128)S(1)} %all_to_all.32.received, f32[10,3,304,128]{3,2,1,0:T(8,128)S(1)} %get-tuple-element.44.state_in), custom_call_target="tpu_custom_call", output_to_operand_aliasing={{1}: (2, {})} | custom-call | tf_op jit(solution)/shard_map/two_steps/pallas_call | solution.py:530
  68.3 13.7 %all_to_all.33.received = f32[128,1,8]{2,1,0:T(1,128)S(1)} all-to-all(f32[128,1,8]{2,1,0:T(1,128)S(1)} %get-tuple-element.46), channel_id=1, replica_groups=mesh['row_0'=2,'row_1'=4,'col_0'=2,'col_1'=4,'col_2'=2] {'row_0','row_1'..., dimensions={0} | all-to-all | bytes 8192 | tf_op jit(solution)/shard_map/all_to_all | solution.py:463
  82.1 1.8 %two_steps.6 = (f32[8,128]{1,0:T(8,128)S(1)}, f32[10,3,304,128]{3,2,1,0:T(8,128)S(1)}, f32[128,1,8]{2,1,0:T(1,128)S(1)}) custom-call(f32[8,128]{1,0:T(8,128)S(1)} %get-tuple-element.45.table, f32[128,1,8]{2,1,0:T(1,128)S(1)} %all_to_all.33.received, f32[10,3,304,128]{3,2,1,0:T(8,128)S(1)} %get-tuple-element.47.state_in), custom_call_target="tpu_custom_call", output_to_operand_aliasing={{1}: (2, {})} | custom-call | tf_op jit(solution)/shard_map/two_steps/pallas_call | solution.py:530
  83.9 13.7 %all_to_all.34.received = f32[128,1,8]{2,1,0:T(1,128)S(1)} all-to-all(f32[128,1,8]{2,1,0:T(1,128)S(1)} %get-tuple-element.49), channel_id=1, replica_groups=mesh['row_0'=2,'row_1'=4,'col_0'=2,'col_1'=4,'col_2'=2] {'row_0','row_1'..., dimensions={0} | all-to-all | bytes 8192 | tf_op jit(solution)/shard_map/all_to_all | solution.py:463
  97.6 2.2 %two_steps.7 = (f32[8,128]{1,0:T(8,128)S(1)}, f32[10,3,304,128]{3,2,1,0:T(8,128)S(1)}, f32[128,1,8]{2,1,0:T(1,128)S(1)}, f32[2,256,256]{2,1,0:T(8,128)}) custom-call(f32[8,128]{1,0:T(8,128)S(1)} %get-tuple-element.48.table, f32[128,1,8]{2,1,0:T(1,128)S(1)} %all_to_all.34.received, ...), custom_call_target="tpu_custom_call", output_to_operand_aliasing={{1}: (2, {})} | custom-call | tf_op jit(solution)/shard_map/two_steps/pallas_call | solution.py:530
  99.8 13.7 %all_to_all.35.received = f32[128,1,8]{2,1,0:T(1,128)S(1)} all-to-all(f32[128,1,8]{2,1,0:T(1,128)S(1)} %get-tuple-element.53), channel_id=1, replica_groups=mesh['row_0'=2,'row_1'=4,'col_0'=2,'col_1'=4,'col_2'=2] {'row_0','row_1'..., dimensions={0} | all-to-all | bytes 8192 | tf_op jit(solution)/shard_map/all_to_all | solution.py:463
  113.6 1.3 %last.1 = (f32[2,256,256]{2,1,0:T(8,128)}, f32[2,2]{1,0:T(2,128)}, f32[2,2]{1,0:T(2,128)}) custom-call(f32[8,128]{1,0:T(8,128)S(1)} %get-tuple-element.52.table, f32[128,1,8]{2,1,0:T(1,128)S(1)} %all_to_all.35.received, f32[10,3,304,128]{3,2,1,0:T(8,128)S(1)} %get-tuple-element.54.state), custom_call_target="tpu_custom_call" | custom-call | tf_op jit(solution)/shard_map/last/pallas_call | solution.py:541
Async XLA Ops:
  2.7 9.8 %collective-permute-start = (f32[256,128]{1,0:T(8,128)S(1)}, f32[256,128]{1,0:T(8,128)S(1)}, u32[]{:S(2)}, u32[]{:S(2)}) collective-permute-start(f32[256,128]{1,0:T(8,128)S(1)} %get-tuple-element.33), channel_id=1, source_target_pairs={{0,15},{1,0},{2,1},{3,2},{4,3},{5,4},{6,5},{7,6},{8,7},{9,8},{10,9... | collective-permute-start | bytes 393224 | tf_op jit(solution)/shard_map/ppermute | solution.py:459
  4.2 8.6 %collective-permute-start.2 = (f32[256,128]{1,0:T(8,128)S(1)}, f32[256,128]{1,0:T(8,128)S(1)}, u32[]{:S(2)}, u32[]{:S(2)}) collective-permute-start(f32[256,128]{1,0:T(8,128)S(1)} %get-tuple-element.35), channel_id=1, source_target_pairs={{0,1},{1,2},{2,3},{3,4},{4,5},{5,6},{6,7},{7,8},{8,9},{9,10},{10,1... | collective-permute-start | bytes 393224 | tf_op jit(solution)/shard_map/ppermute | solution.py:459
  5.5 7.0 %collective-permute-start.1 = (f32[2,256]{1,0:T(2,128)S(1)}, f32[2,256]{1,0:T(2,128)S(1)}, u32[]{:S(2)}, u32[]{:S(2)}) collective-permute-start(f32[2,256]{1,0:T(2,128)S(1)} %get-tuple-element.34), channel_id=1, source_target_pairs={{0,112},{16,0},{32,16},{48,32},{64,48},{80,64},{96,80},{112,96},{1... | collective-permute-start | bytes 6152 | tf_op jit(solution)/shard_map/ppermute | solution.py:459
  13.2 22.2 %collective-permute-start.3 = (f32[112,256]{1,0:T(8,128)S(1)}, f32[112,256]{1,0:T(8,128)S(1)}, u32[]{:S(2)}, u32[]{:S(2)}) collective-permute-start(f32[112,256]{1,0:T(8,128)S(1)} %get-tuple-element.36), channel_id=1, source_target_pairs={{0,16},{16,32},{32,48},{48,64},{64,80},{80,96},{96,112},{112,0},{1... | collective-permute-start | bytes 344072 | tf_op jit(solution)/shard_map/ppermute | solution.py:459
  13.3 22.1 %collective-permute-start.4 = (f32[112,256]{1,0:T(8,128)S(1)}, f32[112,256]{1,0:T(8,128)S(1)}, u32[]{:S(2)}, u32[]{:S(2)}) collective-permute-start(f32[112,256]{1,0:T(8,128)S(1)} %get-tuple-element.37), channel_id=1, source_target_pairs={{0,112},{16,0},{32,16},{48,32},{64,48},{80,64},{96,80},{112,96},{1... | collective-permute-start | bytes 344072 | tf_op jit(solution)/shard_map/ppermute | solution.py:459

commit v4 on v3

--- a/solution.py
+++ b/solution.py
@@ -17,9 +17,12 @@
 HALO = 16
 GUARD = 8
 TOP = GUARD + HALO
-ROWS = 2 * TOP + SIZE
+ROWS = 2 * TOP + SIZE + 8
 END = TOP + SIZE
-FIELDS = 6
+DEPTHS = (12, 12, 10, 10, 10, 10)
+STARTS = (0, 12, 24, 34, 44, 54)
+HALF = SIZE // 2
+STRIP = 72
 PIECES = 4
 SHIFT = 8.0
 VMEM = pl.BlockSpec(memory_space=pltpu.VMEM)
@@ -145,20 +148,49 @@
 
 
 def put_sums(out, values):
-    lane = lax.broadcasted_iota(jnp.int32, (1, 8), 1)
-    row = jnp.zeros((1, 8), F32)
+    lane = lax.broadcasted_iota(jnp.int32, (1, 128), 1)
+    row = jnp.zeros((1, 128), F32)
     for i, value in enumerate(values):
         total = jnp.sum(jnp.sum(value, axis=0, keepdims=True), axis=1, keepdims=True)
         row = jnp.where(lane == i, total, row)
-    out[...] = jnp.broadcast_to(row[None], out.shape)
+    out[...] = jnp.broadcast_to(row, out.shape)
 
 
 OFFSET, SCALE, SPEED_0, SPEED_1, STEP, COUNT = range(6)
+
+
+def turned(value, shift):
+    return value if shift % 128 == 0 else pltpu.roll(value, shift % 128, 1)
+
+
+def even_row():
+    return lax.axis_index(ROW[-1]) % 2 == 0
+
+
+def even_column():
+    return lax.axis_index(COL[-1]) % 2 == 0
+
+
+def pack_columns(parts, tile, row, lane):
+    packed = jnp.zeros((8, 128), F32)
+    for half in range(2):
+        for part, depth, start in zip(parts, DEPTHS, STARTS, strict=True):
+            first = 64 * half + start
+            value = part[tile, pl.ds(TOP + HALF * half + row, 8), :]
+            inside = (lane >= first) & (lane < first + depth)
+            packed = jnp.where(inside, turned(value, first + tile * depth), packed)
+    return packed
+
+
+def pack_rows(out, parts, row, skips):
+    for part, depth, start, skip in zip(parts, DEPTHS, STARTS, skips, strict=True):
+        for i in range(2):
+            out[pl.ds(start, depth), pl.ds(128 * i, 128)] = part[i, pl.ds(row + skip, depth), :]
 
 
 def load_kernel(
     latent, momentum, counts_in, kappa_in, hyper, speed, size,
-    state, left, right, low, table, raw, small, sems,
+    state, inner, outer, low, table, raw, small, sems,
 ):
     field, moment, counts, kappa, _, _ = views(state)
     copies = [(hyper, small.at[pl.ds(0, 2)]), (speed, small.at[pl.ds(2, 2)])]
@@ -177,41 +209,30 @@
     for copy in copies:
         copy.wait()
     lane = lanes()
-    group = lane // HALO
+    parts = parts_of(state)
 
     def body(row, carry):
         here = pl.ds(row - TOP, 8)
         own = pl.ds(row, 8)
-        for out, tile, base in ((left, 0, 0), (right, 1, HALO)):
-            count = raw[tile, here, :].astype(F32)
-            counts[tile, own, :] = count
-            diagonal = kappa[tile, own, :] + 4.0
-            kappa[tile, own, :] = diagonal
-            parts = [
-                field[0, tile, own, :],
-                field[1, tile, own, :],
-                moment[0, tile, own, :],
-                moment[1, tile, own, :],
-                count,
-                diagonal,
-            ]
-            packed = jnp.zeros((8, 128), F32)
-            for n, part in enumerate(parts):
-                shift = (HALO * n + base) % 128
-                moved = part if shift == 0 else pltpu.roll(part, shift, 1)
-                packed = jnp.where(group == n, moved, packed)
-            out[here, :] = packed
+        for i in range(2):
+            counts[i, own, :] = raw[i, here, :].astype(F32)
+            kappa[i, own, :] += 4.0
         return carry
 
     loop(TOP, END, body, ())
     for c in range(2):
         for i in range(2):
             low[pl.ds(c, 1), pl.ds(128 * i, 128)] = field[c, i, pl.ds(TOP, 1), :]
+    even = even_column()
+    for row in range(0, HALF, 8):
+        left, right = (pack_columns(parts, tile, row, lane) for tile in range(2))
+        inner[pl.ds(row, 8), :] = jnp.where(even, right, left)
+        outer[pl.ds(row, 8), :] = jnp.where(even, left, right)
     table[...] = jnp.zeros((8, 128), F32)
     table[pl.ds(0, 5), pl.ds(0, 2)] = small[...]
 
 
-def local_sums_kernel(table, state, partial):
+def local_sums_kernel(table, state, partial, up, down):
     field, _, counts, kappa, _, _ = views(state)
     lane = lanes()
     offset = table[pl.ds(OFFSET, 1), pl.ds(0, 2)]
@@ -235,87 +256,96 @@
         return tuple(carry)
 
     put_sums(partial, loop(TOP, END, body, zeros(5)))
-
-
-def edges_kernel(state, from_right, below, partial, spread):
+    pack_rows(up, parts_of(state), TOP, [0] * 6)
+    pack_rows(down, parts_of(state), END - HALO, [HALO - depth for depth in DEPTHS])
+
+
+def parts_of(state):
+    field, moment, counts, kappa, _, _ = views(state)
+    return [field.at[0], field.at[1], moment.at[0], moment.at[1], counts, kappa]
+
+
+def unpack(from_right, from_left, lane, n, right_at, left_at):
+    depth = DEPTHS[n]
+    right = turned(from_right, -right_at - STARTS[n])
+    left = turned(from_left, -depth - left_at - STARTS[n])
+    return jnp.where(lane < depth, right, jnp.where(lane >= 128 - depth, left, 0.0))
+
+
+def join_kernel(
+    state_in, col_inner, col_outer, below, partial, up, down, state, spread, inner, outer
+):
+    del state_in
+    even = even_column()
+    lane = lanes()
+    parts = parts_of(state)
     field = views(state)[0]
-    lane = lanes()
-
-    def body(row, carry):
-        carry = list(carry)
-        buffer = from_right[pl.ds(row - TOP, 8), :]
-        for c in range(2):
-            other = buffer if c == 0 else pltpu.roll(buffer, 128 - HALO * c, 1)
-            edge = pltpu.roll(field[c, 1, pl.ds(row, 8), :], 1, 1) * other
-            carry[c] += jnp.where(lane == 0, edge, 0.0)
-        return tuple(carry)
-
-    edges = loop(TOP, END, body, zeros(2))
-    index = lax.broadcasted_iota(jnp.int32, (1, 8), 1)
-    row = partial[0]
+    edges = list(zeros(2))
+    for half in range(2):
+        for row in range(0, HALF, 8):
+            a, b = col_inner[pl.ds(row, 8), :], col_outer[pl.ds(row, 8), :]
+            right, left = jnp.where(even, a, b), jnp.where(even, b, a)
+            own = pl.ds(TOP + HALF * half + row, 8)
+            for n, part in enumerate(parts):
+                tile = unpack(right, left, lane, n, 64 * half, 64 * half)
+                part[2, own, :] = tile
+                if n < 2:
+                    edge = pltpu.roll(part[1, own, :], 1, 1) * tile
+                    edges[n] += jnp.where(lane == 0, edge, 0.0)
+    even_r = even_row()
+
+    def put(rows, cols, high, low):
+        inner[rows, cols] = jnp.where(even_r, low, high)
+        outer[rows, cols] = jnp.where(even_r, high, low)
+
+    for i in range(2):
+        cols = pl.ds(128 * i, 128)
+        for row in range(0, 64, 8):
+            rows = pl.ds(row, 8)
+            put(rows, cols, up[rows, cols], down[rows, cols])
+        top, end = pl.ds(8 * i, 8), pl.ds(HALF - HALO + 8 * i, 8)
+        (right, low_right), (left, low_left) = (
+            [jnp.where(even, p[rows, :], q[rows, :]) for rows in (top, end)]
+            for p, q in ((col_inner, col_outer), (col_outer, col_inner))
+        )
+        high = jnp.where(lane < 64, right, pltpu.roll(left, 64, 1))
+        low = jnp.where(lane < 64, pltpu.roll(low_right, 64, 1), low_left)
+        put(pl.ds(64, 8), cols, high, low)
+    index = lax.broadcasted_iota(jnp.int32, (1, 128), 1)
+    result = partial[pl.ds(0, 1), :]
     for c in range(2):
         total = jnp.sum(jnp.sum(edges[c], axis=0, keepdims=True), axis=1, keepdims=True)
         for i in range(2):
             own = field[c, i, pl.ds(END - 1, 1), :]
             other = below[pl.ds(c, 1), pl.ds(128 * i, 128)]
             total += jnp.sum(own * other, axis=1, keepdims=True)
-        row -= jnp.where(index == c, 2.0 * total, 0.0)
-    spread[...] = jnp.broadcast_to(row[None], spread.shape)
-
-
-def unpack(buffers, lane, n):
-    from_right, from_left = buffers
-    near = HALO * n % 128
-    far = (HALO * n + HALO) % 128
-    a = from_right if near == 0 else pltpu.roll(from_right, 128 - near, 1)
-    b = from_left if far == 0 else pltpu.roll(from_left, 128 - far, 1)
-    return jnp.where(lane < HALO, a, jnp.where(lane >= 128 - HALO, b, 0.0))
-
-
-def parts_of(state):
-    field, moment, counts, kappa, _, _ = views(state)
-    return [field.at[0], field.at[1], moment.at[0], moment.at[1], counts, kappa]
-
-
-def columns_kernel(state_in, from_right, from_left, state, up, down):
-    del state_in
+        result -= jnp.where(index == c, 2.0 * total, 0.0)
+    spread[...] = jnp.broadcast_to(result, spread.shape)
+
+
+def unpack_rows(inner, outer, state):
     lane = lanes()
     parts = parts_of(state)
-
-    def body(row, carry):
-        here = pl.ds(row - TOP, 8)
-        buffers = (from_right[here, :], from_left[here, :])
+    even = even_row()
+
+    def both(*at):
+        a, b = inner[at], outer[at]
+        return jnp.where(even, b, a), jnp.where(even, a, b)
+
+    for n, (part, depth, start) in enumerate(zip(parts, DEPTHS, STARTS, strict=True)):
+        for i in range(2):
+            above, below = both(pl.ds(start, depth), pl.ds(128 * i, 128))
+            part[i, pl.ds(TOP - depth, depth), :] = above
+            part[i, pl.ds(END, depth), :] = below
+    for i in range(2):
+        above, below = both(pl.ds(64, 8), pl.ds(128 * i, 128))
         for n, part in enumerate(parts):
-            part[2, pl.ds(row, 8), :] = unpack(buffers, lane, n)
-        return carry
-
-    loop(TOP, END, body, ())
-    for out, row, here in ((up, TOP, 0), (down, END - HALO, SIZE - HALO)):
-        for n, part in enumerate(parts):
-            for i in range(2):
-                out[pl.ds(HALO * n, HALO), pl.ds(128 * i, 128)] = part[i, pl.ds(row, HALO), :]
-        corner = pl.ds(HALO * FIELDS, HALO)
-        out[corner, pl.ds(0, 128)] = from_right[pl.ds(here, HALO), :]
-        out[corner, pl.ds(128, 128)] = from_left[pl.ds(here, HALO), :]
-
-
-def unpack_rows(from_above, from_below, state):
-    lane = lanes()
-    parts = parts_of(state)
-    for buffer, row in ((from_above, GUARD), (from_below, END)):
-        for block in range(0, HALO, 8):
-            corner = pl.ds(HALO * FIELDS + block, 8)
-            buffers = (buffer[corner, pl.ds(0, 128)], buffer[corner, pl.ds(128, 128)])
-            for n, part in enumerate(parts):
-                for i in range(2):
-                    part[i, pl.ds(row + block, 8), :] = buffer[
-                        pl.ds(HALO * n + block, 8), pl.ds(128 * i, 128)
-                    ]
-                part[2, pl.ds(row + block, 8), :] = unpack(buffers, lane, n)
+            part[2, pl.ds(GUARD + 8 * i, 8), :] = unpack(above, above, lane, n, 0, 64)
+            part[2, pl.ds(END + 8 * i, 8), :] = unpack(below, below, lane, n, 0, 64)
 
 
 def sum_of(received):
-    return jnp.sum(received[...], axis=0)
+    return jnp.sum(received[...], axis=0, keepdims=True)
 
 
 def read_table(table):
@@ -333,10 +363,10 @@
 
 
 def first_step_kernel(
-    total, table, received, from_above, from_below, state_in, table_out, state, partial, other
+    total, table, received, inner, outer, state_in, table_out, state, partial, other
 ):
     del state_in
-    unpack_rows(from_above, from_below, state)
+    unpack_rows(inner, outer, state)
     field, moment, counts, kappa, slope, growth = views(state)
     reduced = sum_of(received)
     offset, scale, speed_0, speed_1, size, _ = read_table(table)
@@ -459,19 +489,28 @@
     return lax.ppermute(x, axes, [(i, (i + step) % count) for i in range(count)])
 
 
+def swap(x, axes, first):
+    count = lax.axis_size(axes)
+    pairs = [((first + i) % count, (first + i + 1) % count) for i in range(0, count, 2)]
+    return lax.ppermute(x, axes, [p for a, b in pairs for p in ((a, b), (b, a))])
+
+
 def exchange(spread):
-    return lax.all_to_all(spread, ALL, 0, 0, tiled=True)
+    shape = spread.shape
+    spread = spread.reshape(shape[0], 1, shape[1])
+    return lax.all_to_all(spread, ALL, 0, 0, tiled=True).reshape(shape)
 
 
 def shards(latent, momentum, hyper_params, velocity, step_size, counts, kappa_field):
     devices = lax.axis_size(ALL)
     total = float(latent.shape[1] * latent.shape[2] * devices)
-    spread = vmem(devices, 1, 8)
+    spread = vmem(devices, 128)
     small_table = jax.ShapeDtypeStruct((8, 128), F32)
     given = (latent, momentum, counts, kappa_field, hyper_params, velocity, step_size[None])
-    state, left, right, low, table = pl.pallas_call(
+    packed, strip = vmem(HALF, 128), vmem(STRIP, SIZE)
+    state, inner, outer, low, table = pl.pallas_call(
         load_kernel,
-        out_shape=(STATE, vmem(SIZE, 128), vmem(SIZE, 128), vmem(2, SIZE), vmem(8, 128)),
+        out_shape=(STATE, packed, packed, vmem(2, SIZE), vmem(8, 128)),
         in_specs=[ANY] * 7,
         out_specs=(VMEM,) * 5,
         scratch_shapes=[
@@ -482,35 +521,26 @@
         compiler_params=PARAMS,
         name="load",
     )(*(pltpu.with_memory_space_constraint(a, pltpu.HBM) for a in given))
-    from_right, from_left = ring(left, COL, -1), ring(right, COL, 1)
     below = ring(low, ROW, -1)
-    partial = pl.pallas_call(
+    inner, outer = swap(inner, COL, 0), swap(outer, COL, 1)
+    partial, up, down = pl.pallas_call(
         local_sums_kernel,
-        out_shape=vmem(1, 1, 8),
+        out_shape=(vmem(8, 128), strip, strip),
         in_specs=[VMEM] * 2,
-        out_specs=VMEM,
+        out_specs=(VMEM,) * 3,
         compiler_params=PARAMS,
         name="local_sums",
     )(held(table), held(state))
-    partial = pl.pallas_call(
-        edges_kernel,
-        out_shape=spread,
-        in_specs=[VMEM] * 4,
-        out_specs=VMEM,
-        compiler_params=PARAMS,
-        name="edges",
-    )(held(state), from_right, below, partial)
-    edge = vmem(HALO * (FIELDS + 1), SIZE)
-    state, up, down = pl.pallas_call(
-        columns_kernel,
-        out_shape=(STATE, edge, edge),
-        in_specs=[VMEM] * 3,
-        out_specs=(VMEM,) * 3,
+    state, partial, row_inner, row_outer = pl.pallas_call(
+        join_kernel,
+        out_shape=(STATE, spread, strip, strip),
+        in_specs=[VMEM] * 7,
+        out_specs=(VMEM,) * 4,
         input_output_aliases={0: 0},
         compiler_params=PARAMS,
-        name="columns",
-    )(held(state), from_right, from_left)
-    from_below, from_above = ring(up, ROW, -1), ring(down, ROW, 1)
+        name="join",
+    )(held(state), inner, outer, below, partial, held(up), held(down))
+    row_inner, row_outer = swap(row_inner, ROW, 0), swap(row_outer, ROW, 1)
     received = exchange(partial)
     table, state, partial = pl.pallas_call(
         functools.partial(first_step_kernel, total),
@@ -521,7 +551,7 @@
         scratch_shapes=[vmem(2, 3, ROWS, 128)],
         compiler_params=PARAMS,
         name="first_steps",
-    )(table, received, from_above, from_below, held(state))
+    )(table, received, row_inner, row_outer, held(state))
     latent_out = ()
     result = jax.ShapeDtypeStruct(latent.shape, F32)
     for index in range(STEPS // 2 - 1):

time: 115 us -> 115 us (level)
    ppermute x0 -> x4, starting transfers between devices: none -> 8.34 us  [swap(): lax.ppermute(x, axes, [p for a, b in pairs for p in ((a, b), (b, a))])]
    ppermute x5 -> x1, starting transfers between devices: 14.5 us -> 6.22 us  [ring(): lax.ppermute(x, axes, [(i, (i + step) % count) for i in range(count)])]
    pallas_call x4 -> x3, Pallas kernels: 3.17 us -> 3.04 us  [the longest x1 2.05 us: shards(): pl.pallas_call(load_kernel, out_shape=(STATE, packed, packed, vmem(2, SIZ...]
  transfers between devices with their start and end apart: 5 -> 5, of which waited for: 1 -> 1; matrix products, arithmetic and copies ran while one was open for 0% -> 0% of each run, Pallas kernels for 1% -> 0%
where the time goes in v4:
time: 115 us; the launch traced here: 114 us
  blocking collectives  85.3 us (74%)
  starting transfers between devices  14.6 us (13%)
  Pallas kernels  13.1 us (11%)
    all_to_all x6, blocking collectives, exchange(): return lax.all_to_all(spread, ALL, 0, 0, tiled=True).reshape(shape)  85.3 us
    ppermute x4, starting transfers between devices, swap(): lax.ppermute(x, axes, [p for a, b in pairs for p in ((a, b), (b, a))])  8.34 us
    pallas_call x4, Pallas kernels, shards(): pl.pallas_call(functools.partial(two_steps_kernel, total, final), out_sha...  7 us
    ppermute x1, starting transfers between devices, ring(): lax.ppermute(x, axes, [(i, (i + step) % count) for i in range(count)])  6.22 us
  transfers between devices with their start and end apart: 5, of which 1 were waited for; matrix products, arithmetic and copies ran while one was open for 0% of the time, Pallas kernels for 0%

profile of v4, /device:TPU:1, one launch (start us, length us, event | category | flops | bytes accessed | tf_op | source)
XLA Modules:
  0.0 114.2 jit_solution(7612886275117034783)
XLA Ops:
  0.6 2.0 %load.1 = (f32[10,3,312,128]{3,2,1,0:T(8,128)S(1)}, f32[128,128]{1,0:T(8,128)S(1)}, f32[128,128]{1,0:T(8,128)S(1)}, f32[2,256]{1,0:T(2,128)S(1)}, f32[8,128]{1,0:T(8,128)S(1)}) custom-call(f32[2,256,256]{2,1,0:T(8,128)} %latent.1, f32[2,256,256]{2,1,0:T(8,128)} %momentum.1, s32[256,256]{1,0:T(8,128)} %counts_in.1, f32[256,256]{1,0:T(8,128)} %kappa_in.1, ...), custom_call_target="tpu_custom_call" | custom-call | tf_op jit(solution)/shard_map/load/pallas_call | solution.py:511
  2.7 1.5 %collective-permute-start = (f32[128,128]{1,0:T(8,128)S(1)}, f32[128,128]{1,0:T(8,128)S(1)}, u32[]{:S(2)}, u32[]{:S(2)}) collective-permute-start(f32[128,128]{1,0:T(8,128)S(1)} %get-tuple-element.37), channel_id=1, source_target_pairs={{0,1},{1,0},{2,3},{3,2},{4,5},{5,4},{6,7},{7,6},{8,9},{9,8},{10,11... | collective-permute-start | bytes 196616 | tf_op jit(solution)/shard_map/ppermute | solution.py:495
  4.2 1.4 %collective-permute-start.1 = (f32[128,128]{1,0:T(8,128)S(1)}, f32[128,128]{1,0:T(8,128)S(1)}, u32[]{:S(2)}, u32[]{:S(2)}) collective-permute-start(f32[128,128]{1,0:T(8,128)S(1)} %get-tuple-element.38), channel_id=1, source_target_pairs={{1,2},{2,1},{3,4},{4,3},{5,6},{6,5},{7,8},{8,7},{9,10},{10,9},{11,... | collective-permute-start | bytes 196616 | tf_op jit(solution)/shard_map/ppermute | solution.py:495
  5.5 6.2 %collective-permute-start.2 = (f32[2,256]{1,0:T(2,128)S(1)}, f32[2,256]{1,0:T(2,128)S(1)}, u32[]{:S(2)}, u32[]{:S(2)}) collective-permute-start(f32[2,256]{1,0:T(2,128)S(1)} %get-tuple-element.39), channel_id=1, source_target_pairs={{0,112},{16,0},{32,16},{48,32},{64,48},{80,64},{96,80},{112,96},{1... | collective-permute-start | bytes 6152 | tf_op jit(solution)/shard_map/ppermute | solution.py:489
  11.8 0.4 local_sums.1
  12.2 0.3 collective-permute-done.2.below
  12.5 0.0 collective-permute-done.col_inner
  12.5 0.0 collective-permute-done.1.col_outer
  12.5 0.6 join.1
  13.1 0.1 collective-permute-start.3
  13.2 5.4 %collective-permute-start.4 = (f32[72,256]{1,0:T(8,128)S(1)}, f32[72,256]{1,0:T(8,128)S(1)}, u32[]{:S(2)}, u32[]{:S(2)}) collective-permute-start(f32[72,256]{1,0:T(8,128)S(1)} %get-tuple-element.45), channel_id=1, source_target_pairs={{16,32},{32,16},{48,64},{64,48},{80,96},{96,80},{112,0},{0,112},{1... | collective-permute-start | bytes 221192 | tf_op jit(solution)/shard_map/ppermute | solution.py:495
  18.6 16.7 %all_to_all.30 = f32[128,1,128]{2,1,0:T(1,128)S(1)} all-to-all(f32[128,1,128]{2,1,0:T(1,128)S(1)} %bitcast.31), channel_id=1, replica_groups=mesh['row_0'=2,'row_1'=4,'col_0'=2,'col_1'=4,'col_2'=2] {'row_0','row_1'..., dimensions={0} | all-to-all | bytes 131072 | tf_op jit(solution)/shard_map/all_to_all | solution.py:501
  35.3 0.0 collective-permute-done.3.inner
  35.3 0.0 collective-permute-done.4.outer
  35.3 1.9 %first_steps.1 = (f32[8,128]{1,0:T(8,128)S(1)}, f32[10,3,312,128]{3,2,1,0:T(8,128)S(1)}, f32[128,128]{1,0:T(8,128)S(1)}) custom-call(f32[8,128]{1,0:T(8,128)S(1)} %get-tuple-element.35.table, f32[128,128]{1,0:T(8,128)S(1)} %bitcast.25, f32[72,256]{1,0:T(8,128)S(1)} %collective-permute-done.3.inner, ...), custom_call_target="tpu_custom_call", output_to_operand_aliasing={{1}: (4, {})} | custom-call | tf_op jit(solution)/shard_map/first_steps/pallas_call | solution.py:545
  37.2 13.7 %all_to_all.31 = f32[128,1,128]{2,1,0:T(1,128)S(1)} all-to-all(f32[128,1,128]{2,1,0:T(1,128)S(1)} %bitcast.32), channel_id=1, replica_groups=mesh['row_0'=2,'row_1'=4,'col_0'=2,'col_1'=4,'col_2'=2] {'row_0','row_1'..., dimensions={0} | all-to-all | bytes 131072 | tf_op jit(solution)/shard_map/all_to_all | solution.py:501
  50.9 1.6 %two_steps.4 = (f32[8,128]{1,0:T(8,128)S(1)}, f32[10,3,312,128]{3,2,1,0:T(8,128)S(1)}, f32[128,128]{1,0:T(8,128)S(1)}) custom-call(f32[8,128]{1,0:T(8,128)S(1)} %get-tuple-element.47.table, f32[128,128]{1,0:T(8,128)S(1)} %bitcast.27, f32[10,3,312,128]{3,2,1,0:T(8,128)S(1)} %get-tuple-element.49.state_in), custom_call_target="tpu_custom_call", output_to_operand_aliasing={{1}: (2, {})} | custom-call | tf_op jit(solution)/shard_map/two_steps/pallas_call | solution.py:560
  52.5 13.7 %all_to_all.32 = f32[128,1,128]{2,1,0:T(1,128)S(1)} all-to-all(f32[128,1,128]{2,1,0:T(1,128)S(1)} %bitcast.34), channel_id=1, replica_groups=mesh['row_0'=2,'row_1'=4,'col_0'=2,'col_1'=4,'col_2'=2] {'row_0','row_1'..., dimensions={0} | all-to-all | bytes 131072 | tf_op jit(solution)/shard_map/all_to_all | solution.py:501
  66.3 1.6 %two_steps.5 = (f32[8,128]{1,0:T(8,128)S(1)}, f32[10,3,312,128]{3,2,1,0:T(8,128)S(1)}, f32[128,128]{1,0:T(8,128)S(1)}) custom-call(f32[8,128]{1,0:T(8,128)S(1)} %get-tuple-element.50.table, f32[128,128]{1,0:T(8,128)S(1)} %bitcast.28, f32[10,3,312,128]{3,2,1,0:T(8,128)S(1)} %get-tuple-element.52.state_in), custom_call_target="tpu_custom_call", output_to_operand_aliasing={{1}: (2, {})} | custom-call | tf_op jit(solution)/shard_map/two_steps/pallas_call | solution.py:560
  67.9 13.7 %all_to_all.33 = f32[128,1,128]{2,1,0:T(1,128)S(1)} all-to-all(f32[128,1,128]{2,1,0:T(1,128)S(1)} %bitcast.35), channel_id=1, replica_groups=mesh['row_0'=2,'row_1'=4,'col_0'=2,'col_1'=4,'col_2'=2] {'row_0','row_1'..., dimensions={0} | all-to-all | bytes 131072 | tf_op jit(solution)/shard_map/all_to_all | solution.py:501
  81.6 1.6 %two_steps.6 = (f32[8,128]{1,0:T(8,128)S(1)}, f32[10,3,312,128]{3,2,1,0:T(8,128)S(1)}, f32[128,128]{1,0:T(8,128)S(1)}) custom-call(f32[8,128]{1,0:T(8,128)S(1)} %get-tuple-element.53.table, f32[128,128]{1,0:T(8,128)S(1)} %bitcast.29, f32[10,3,312,128]{3,2,1,0:T(8,128)S(1)} %get-tuple-element.55.state_in), custom_call_target="tpu_custom_call", output_to_operand_aliasing={{1}: (2, {})} | custom-call | tf_op jit(solution)/shard_map/two_steps/pallas_call | solution.py:560
  83.3 13.7 %all_to_all.34 = f32[128,1,128]{2,1,0:T(1,128)S(1)} all-to-all(f32[128,1,128]{2,1,0:T(1,128)S(1)} %bitcast.36), channel_id=1, replica_groups=mesh['row_0'=2,'row_1'=4,'col_0'=2,'col_1'=4,'col_2'=2] {'row_0','row_1'..., dimensions={0} | all-to-all | bytes 131072 | tf_op jit(solution)/shard_map/all_to_all | solution.py:501
  97.0 2.1 %two_steps.7 = (f32[8,128]{1,0:T(8,128)S(1)}, f32[10,3,312,128]{3,2,1,0:T(8,128)S(1)}, f32[128,128]{1,0:T(8,128)S(1)}, f32[2,256,256]{2,1,0:T(8,128)}) custom-call(f32[8,128]{1,0:T(8,128)S(1)} %get-tuple-element.56.table, f32[128,128]{1,0:T(8,128)S(1)} %bitcast.26, f32[10,3,312,128]{3,2,1,0:T(8,128)S(1)} %get-tuple-element.58.state_in), custom_call_target="tpu_custom_call", output_to_operand_aliasing={{1}: (2, {})} | custom-call | tf_op jit(solution)/shard_map/two_steps/pallas_call | solution.py:560
  99.1 13.7 %all_to_all.35 = f32[128,1,128]{2,1,0:T(1,128)S(1)} all-to-all(f32[128,1,128]{2,1,0:T(1,128)S(1)} %bitcast.33), channel_id=1, replica_groups=mesh['row_0'=2,'row_1'=4,'col_0'=2,'col_1'=4,'col_2'=2] {'row_0','row_1'..., dimensions={0} | all-to-all | bytes 131072 | tf_op jit(solution)/shard_map/all_to_all | solution.py:501
  112.8 1.2 %last.1 = (f32[2,256,256]{2,1,0:T(8,128)}, f32[2,2]{1,0:T(2,128)}, f32[2,2]{1,0:T(2,128)}) custom-call(f32[8,128]{1,0:T(8,128)S(1)} %get-tuple-element.60.table, f32[128,128]{1,0:T(8,128)S(1)} %bitcast.30, f32[10,3,312,128]{3,2,1,0:T(8,128)S(1)} %get-tuple-element.62.state), custom_call_target="tpu_custom_call" | custom-call | tf_op jit(solution)/shard_map/last/pallas_call | solution.py:571
Async XLA Ops:
  2.7 9.8 %collective-permute-start = (f32[128,128]{1,0:T(8,128)S(1)}, f32[128,128]{1,0:T(8,128)S(1)}, u32[]{:S(2)}, u32[]{:S(2)}) collective-permute-start(f32[128,128]{1,0:T(8,128)S(1)} %get-tuple-element.37), channel_id=1, source_target_pairs={{0,1},{1,0},{2,3},{3,2},{4,5},{5,4},{6,7},{7,6},{8,9},{9,8},{10,11... | collective-permute-start | bytes 196616 | tf_op jit(solution)/shard_map/ppermute | solution.py:495
  4.2 8.3 %collective-permute-start.1 = (f32[128,128]{1,0:T(8,128)S(1)}, f32[128,128]{1,0:T(8,128)S(1)}, u32[]{:S(2)}, u32[]{:S(2)}) collective-permute-start(f32[128,128]{1,0:T(8,128)S(1)} %get-tuple-element.38), channel_id=1, source_target_pairs={{1,2},{2,1},{3,4},{4,3},{5,6},{6,5},{7,8},{8,7},{9,10},{10,9},{11,... | collective-permute-start | bytes 196616 | tf_op jit(solution)/shard_map/ppermute | solution.py:495
  5.5 7.0 %collective-permute-start.2 = (f32[2,256]{1,0:T(2,128)S(1)}, f32[2,256]{1,0:T(2,128)S(1)}, u32[]{:S(2)}, u32[]{:S(2)}) collective-permute-start(f32[2,256]{1,0:T(2,128)S(1)} %get-tuple-element.39), channel_id=1, source_target_pairs={{0,112},{16,0},{32,16},{48,32},{64,48},{80,64},{96,80},{112,96},{1... | collective-permute-start | bytes 6152 | tf_op jit(solution)/shard_map/ppermute | solution.py:489
  13.1 22.2 %collective-permute-start.3 = (f32[72,256]{1,0:T(8,128)S(1)}, f32[72,256]{1,0:T(8,128)S(1)}, u32[]{:S(2)}, u32[]{:S(2)}) collective-permute-start(f32[72,256]{1,0:T(8,128)S(1)} %get-tuple-element.44), channel_id=1, source_target_pairs={{0,16},{16,0},{32,48},{48,32},{64,80},{80,64},{96,112},{112,96},{1... | collective-permute-start | bytes 221192 | tf_op jit(solution)/shard_map/ppermute | solution.py:495
  13.2 22.1 %collective-permute-start.4 = (f32[72,256]{1,0:T(8,128)S(1)}, f32[72,256]{1,0:T(8,128)S(1)}, u32[]{:S(2)}, u32[]{:S(2)}) collective-permute-start(f32[72,256]{1,0:T(8,128)S(1)} %get-tuple-element.45), channel_id=1, source_target_pairs={{16,32},{32,16},{48,64},{64,48},{80,96},{96,80},{112,0},{0,112},{1... | collective-permute-start | bytes 221192 | tf_op jit(solution)/shard_map/ppermute | solution.py:495

commit v5 on v4

--- a/solution.py
+++ b/solution.py
@@ -395,8 +395,8 @@
     return offset, scale, speed_0, speed_1, size, count, a_0, a_1, factor
 
 
-def field_copies(field, out, sems):
-    pairs = [(c, i) for c in range(2) for i in range(2)]
+def field_copies(field, out, sems, first):
+    pairs = [(c, i) for c in ((0,) if first else (1,)) for i in range(2)]
     return [
         pltpu.make_async_copy(
             field.at[c, i, pl.ds(TOP, SIZE), :], out.at[c, :, pl.ds(128 * i, 128)], sems.at[n]
@@ -420,7 +420,7 @@
     near = advance(other, field, moment, counts, kappa, offset, jnp.exp(scale), size, 1.0, HALO // 2)
     copies = []
     if final:
-        copies = field_copies(field, latent_out[0], more[-1])
+        copies = field_copies(field, latent_out[0], more[-1], True)
         for copy in copies:
             copy.start()
     far = examine(field, kappa, slope, growth, offset - SHIFT, HALO // 2)
@@ -431,8 +431,13 @@
 
 
 def last_kernel(
-    total, table, received, state, momentum_out, hyper_out, velocity_out, result, small, sems
+    total, table, received, state, latent_in,
+    momentum_out, hyper_out, velocity_out, latent_out, result, small, sems, field_sems,
 ):
+    del latent_in
+    field_out = field_copies(views(state)[0], latent_out, field_sems, False)
+    for copy in field_out:
+        copy.start()
     _, moment, counts, _, slope, growth = views(state)
     offset, scale, speed_0, speed_1, size, _, a_0, a_1, factor = two_params(table, received, total)
     tau = jnp.exp(scale)
@@ -468,7 +473,7 @@
                 )
             )
             copies[-1].start()
-    for copy in copies:
+    for copy in (*field_out, *copies):
         copy.wait()
 
 
@@ -563,29 +568,32 @@
             in_specs=[VMEM] * 3,
             out_specs=(VMEM,) * 3 + final * (ANY,),
             input_output_aliases={2: 1},
-            scratch_shapes=[vmem(2, 3, ROWS, 128)] + final * [pltpu.SemaphoreType.DMA((4,))],
+            scratch_shapes=[vmem(2, 3, ROWS, 128)] + final * [pltpu.SemaphoreType.DMA((2,))],
             compiler_params=PARAMS,
             name="two_steps",
         )(table, received, held(state))
     received = exchange(partial)
-    momentum_out, hyper_out, velocity_out = pl.pallas_call(
+    momentum_out, hyper_out, velocity_out, latent_out = pl.pallas_call(
         functools.partial(last_kernel, total),
         out_shape=(
             result,
             jax.ShapeDtypeStruct((2, 2), F32),
             jax.ShapeDtypeStruct((2, 2), F32),
+            result,
         ),
-        in_specs=[VMEM] * 3,
-        out_specs=(ANY,) * 3,
+        in_specs=[VMEM] * 3 + [ANY],
+        out_specs=(ANY,) * 4,
+        input_output_aliases={3: 3},
         scratch_shapes=[
             vmem(*latent.shape),
             vmem(2, 2, 2),
             pltpu.SemaphoreType.DMA((2 * PIECES + 2,)),
+            pltpu.SemaphoreType.DMA((2,)),
         ],
         compiler_params=PARAMS,
         name="last",
-    )(table, received, held(state))
-    return latent_out[0], momentum_out, hyper_out, velocity_out
+    )(table, received, held(state), latent_out[0])
+    return latent_out, momentum_out, hyper_out, velocity_out
 
 
 def solution(mesh):

time: 115 us -> 114 us (level)
  no operation moved by 1% of the time
where the time goes in v5:
time: 114 us
  blocking collectives  85.3 us (75%)
  starting transfers between devices  14.6 us (13%)
  Pallas kernels  13 us (11%)
    all_to_all x6, blocking collectives, exchange(): return lax.all_to_all(spread, ALL, 0, 0, tiled=True).reshape(shape)  85.3 us
    ppermute x4, starting transfers between devices, swap(): lax.ppermute(x, axes, [p for a, b in pairs for p in ((a, b), (b, a))])  8.34 us
    pallas_call x4, Pallas kernels, shards(): pl.pallas_call(functools.partial(two_steps_kernel, total, final), out_sha...  6.9 us
    ppermute x1, starting transfers between devices, ring(): lax.ppermute(x, axes, [(i, (i + step) % count) for i in range(count)])  6.22 us
  transfers between devices with their start and end apart: 5, of which 1 were waited for; matrix products, arithmetic and copies ran while one was open for 0% of the time, Pallas kernels for 0%

profile of v5, /device:TPU:1, one launch (start us, length us, event | category | flops | bytes accessed | tf_op | source)
XLA Modules:
  0.0 114.1 jit_solution(4596089977802650471)
XLA Ops:
  0.6 2.0 %load.1 = (f32[10,3,312,128]{3,2,1,0:T(8,128)S(1)}, f32[128,128]{1,0:T(8,128)S(1)}, f32[128,128]{1,0:T(8,128)S(1)}, f32[2,256]{1,0:T(2,128)S(1)}, f32[8,128]{1,0:T(8,128)S(1)}) custom-call(f32[2,256,256]{2,1,0:T(8,128)} %latent.1, f32[2,256,256]{2,1,0:T(8,128)} %momentum.1, s32[256,256]{1,0:T(8,128)} %counts_in.1, f32[256,256]{1,0:T(8,128)} %kappa_in.1, ...), custom_call_target="tpu_custom_call" | custom-call | tf_op jit(solution)/shard_map/load/pallas_call | solution.py:516
  2.7 1.5 %collective-permute-start = (f32[128,128]{1,0:T(8,128)S(1)}, f32[128,128]{1,0:T(8,128)S(1)}, u32[]{:S(2)}, u32[]{:S(2)}) collective-permute-start(f32[128,128]{1,0:T(8,128)S(1)} %get-tuple-element.38), channel_id=1, source_target_pairs={{0,1},{1,0},{2,3},{3,2},{4,5},{5,4},{6,7},{7,6},{8,9},{9,8},{10,11... | collective-permute-start | bytes 196616 | tf_op jit(solution)/shard_map/ppermute | solution.py:500
  4.2 1.4 %collective-permute-start.1 = (f32[128,128]{1,0:T(8,128)S(1)}, f32[128,128]{1,0:T(8,128)S(1)}, u32[]{:S(2)}, u32[]{:S(2)}) collective-permute-start(f32[128,128]{1,0:T(8,128)S(1)} %get-tuple-element.39), channel_id=1, source_target_pairs={{1,2},{2,1},{3,4},{4,3},{5,6},{6,5},{7,8},{8,7},{9,10},{10,9},{11,... | collective-permute-start | bytes 196616 | tf_op jit(solution)/shard_map/ppermute | solution.py:500
  5.5 6.2 %collective-permute-start.2 = (f32[2,256]{1,0:T(2,128)S(1)}, f32[2,256]{1,0:T(2,128)S(1)}, u32[]{:S(2)}, u32[]{:S(2)}) collective-permute-start(f32[2,256]{1,0:T(2,128)S(1)} %get-tuple-element.40), channel_id=1, source_target_pairs={{0,112},{16,0},{32,16},{48,32},{64,48},{80,64},{96,80},{112,96},{1... | collective-permute-start | bytes 6152 | tf_op jit(solution)/shard_map/ppermute | solution.py:494
  11.8 0.4 local_sums.1
  12.2 0.3 collective-permute-done.2.below
  12.5 0.0 collective-permute-done.col_inner
  12.5 0.0 collective-permute-done.1.col_outer
  12.5 0.6 join.1
  13.1 0.1 collective-permute-start.3
  13.2 5.4 %collective-permute-start.4 = (f32[72,256]{1,0:T(8,128)S(1)}, f32[72,256]{1,0:T(8,128)S(1)}, u32[]{:S(2)}, u32[]{:S(2)}) collective-permute-start(f32[72,256]{1,0:T(8,128)S(1)} %get-tuple-element.46), channel_id=1, source_target_pairs={{16,32},{32,16},{48,64},{64,48},{80,96},{96,80},{112,0},{0,112},{1... | collective-permute-start | bytes 221192 | tf_op jit(solution)/shard_map/ppermute | solution.py:500
  18.6 16.7 %all_to_all.30 = f32[128,1,128]{2,1,0:T(1,128)S(1)} all-to-all(f32[128,1,128]{2,1,0:T(1,128)S(1)} %bitcast.31), channel_id=1, replica_groups=mesh['row_0'=2,'row_1'=4,'col_0'=2,'col_1'=4,'col_2'=2] {'row_0','row_1'..., dimensions={0} | all-to-all | bytes 131072 | tf_op jit(solution)/shard_map/all_to_all | solution.py:506
  35.3 0.0 collective-permute-done.3.inner
  35.3 0.0 collective-permute-done.4.outer
  35.3 1.9 %first_steps.1 = (f32[8,128]{1,0:T(8,128)S(1)}, f32[10,3,312,128]{3,2,1,0:T(8,128)S(1)}, f32[128,128]{1,0:T(8,128)S(1)}) custom-call(f32[8,128]{1,0:T(8,128)S(1)} %get-tuple-element.36.table, f32[128,128]{1,0:T(8,128)S(1)} %bitcast.25, f32[72,256]{1,0:T(8,128)S(1)} %collective-permute-done.3.inner, ...), custom_call_target="tpu_custom_call", output_to_operand_aliasing={{1}: (4, {})} | custom-call | tf_op jit(solution)/shard_map/first_steps/pallas_call | solution.py:550
  37.2 13.7 %all_to_all.31 = f32[128,1,128]{2,1,0:T(1,128)S(1)} all-to-all(f32[128,1,128]{2,1,0:T(1,128)S(1)} %bitcast.32), channel_id=1, replica_groups=mesh['row_0'=2,'row_1'=4,'col_0'=2,'col_1'=4,'col_2'=2] {'row_0','row_1'..., dimensions={0} | all-to-all | bytes 131072 | tf_op jit(solution)/shard_map/all_to_all | solution.py:506
  50.9 1.6 %two_steps.4 = (f32[8,128]{1,0:T(8,128)S(1)}, f32[10,3,312,128]{3,2,1,0:T(8,128)S(1)}, f32[128,128]{1,0:T(8,128)S(1)}) custom-call(f32[8,128]{1,0:T(8,128)S(1)} %get-tuple-element.48.table, f32[128,128]{1,0:T(8,128)S(1)} %bitcast.28, f32[10,3,312,128]{3,2,1,0:T(8,128)S(1)} %get-tuple-element.50.state_in), custom_call_target="tpu_custom_call", output_to_operand_aliasing={{1}: (2, {})} | custom-call | tf_op jit(solution)/shard_map/two_steps/pallas_call | solution.py:565
  52.5 13.7 %all_to_all.32 = f32[128,1,128]{2,1,0:T(1,128)S(1)} all-to-all(f32[128,1,128]{2,1,0:T(1,128)S(1)} %bitcast.34), channel_id=1, replica_groups=mesh['row_0'=2,'row_1'=4,'col_0'=2,'col_1'=4,'col_2'=2] {'row_0','row_1'..., dimensions={0} | all-to-all | bytes 131072 | tf_op jit(solution)/shard_map/all_to_all | solution.py:506
  66.3 1.6 %two_steps.5 = (f32[8,128]{1,0:T(8,128)S(1)}, f32[10,3,312,128]{3,2,1,0:T(8,128)S(1)}, f32[128,128]{1,0:T(8,128)S(1)}) custom-call(f32[8,128]{1,0:T(8,128)S(1)} %get-tuple-element.51.table, f32[128,128]{1,0:T(8,128)S(1)} %bitcast.29, f32[10,3,312,128]{3,2,1,0:T(8,128)S(1)} %get-tuple-element.53.state_in), custom_call_target="tpu_custom_call", output_to_operand_aliasing={{1}: (2, {})} | custom-call | tf_op jit(solution)/shard_map/two_steps/pallas_call | solution.py:565
  67.9 13.7 %all_to_all.33 = f32[128,1,128]{2,1,0:T(1,128)S(1)} all-to-all(f32[128,1,128]{2,1,0:T(1,128)S(1)} %bitcast.35), channel_id=1, replica_groups=mesh['row_0'=2,'row_1'=4,'col_0'=2,'col_1'=4,'col_2'=2] {'row_0','row_1'..., dimensions={0} | all-to-all | bytes 131072 | tf_op jit(solution)/shard_map/all_to_all | solution.py:506
  81.6 1.6 %two_steps.6 = (f32[8,128]{1,0:T(8,128)S(1)}, f32[10,3,312,128]{3,2,1,0:T(8,128)S(1)}, f32[128,128]{1,0:T(8,128)S(1)}) custom-call(f32[8,128]{1,0:T(8,128)S(1)} %get-tuple-element.54.table, f32[128,128]{1,0:T(8,128)S(1)} %bitcast.30, f32[10,3,312,128]{3,2,1,0:T(8,128)S(1)} %get-tuple-element.56.state_in), custom_call_target="tpu_custom_call", output_to_operand_aliasing={{1}: (2, {})} | custom-call | tf_op jit(solution)/shard_map/two_steps/pallas_call | solution.py:565
  83.3 13.7 %all_to_all.34 = f32[128,1,128]{2,1,0:T(1,128)S(1)} all-to-all(f32[128,1,128]{2,1,0:T(1,128)S(1)} %bitcast.36), channel_id=1, replica_groups=mesh['row_0'=2,'row_1'=4,'col_0'=2,'col_1'=4,'col_2'=2] {'row_0','row_1'..., dimensions={0} | all-to-all | bytes 131072 | tf_op jit(solution)/shard_map/all_to_all | solution.py:506
  97.0 2.0 %two_steps.7 = (f32[8,128]{1,0:T(8,128)S(1)}, f32[10,3,312,128]{3,2,1,0:T(8,128)S(1)}, f32[128,128]{1,0:T(8,128)S(1)}, f32[2,256,256]{2,1,0:T(8,128)}) custom-call(f32[8,128]{1,0:T(8,128)S(1)} %get-tuple-element.57.table, f32[128,128]{1,0:T(8,128)S(1)} %bitcast.27, f32[10,3,312,128]{3,2,1,0:T(8,128)S(1)} %get-tuple-element.59.state_in), custom_call_target="tpu_custom_call", output_to_operand_aliasing={{1}: (2, {})} | custom-call | tf_op jit(solution)/shard_map/two_steps/pallas_call | solution.py:565
  99.0 13.7 %all_to_all.35 = f32[128,1,128]{2,1,0:T(1,128)S(1)} all-to-all(f32[128,1,128]{2,1,0:T(1,128)S(1)} %bitcast.33), channel_id=1, replica_groups=mesh['row_0'=2,'row_1'=4,'col_0'=2,'col_1'=4,'col_2'=2] {'row_0','row_1'..., dimensions={0} | all-to-all | bytes 131072 | tf_op jit(solution)/shard_map/all_to_all | solution.py:506
  112.7 1.2 %last.1 = (f32[2,256,256]{2,1,0:T(8,128)}, f32[2,2]{1,0:T(2,128)}, f32[2,2]{1,0:T(2,128)}, f32[2,256,256]{2,1,0:T(8,128)}) custom-call(f32[8,128]{1,0:T(8,128)S(1)} %get-tuple-element.60.table, f32[128,128]{1,0:T(8,128)S(1)} %bitcast.26, f32[10,3,312,128]{3,2,1,0:T(8,128)S(1)} %get-tuple-element.62.state, ...), custom_call_target="tpu_custom_call", output_to_operand_aliasing={{3}: (3, {})} | custom-call | tf_op jit(solution)/shard_map/last/pallas_call | solution.py:576
Async XLA Ops:
  2.7 9.8 %collective-permute-start = (f32[128,128]{1,0:T(8,128)S(1)}, f32[128,128]{1,0:T(8,128)S(1)}, u32[]{:S(2)}, u32[]{:S(2)}) collective-permute-start(f32[128,128]{1,0:T(8,128)S(1)} %get-tuple-element.38), channel_id=1, source_target_pairs={{0,1},{1,0},{2,3},{3,2},{4,5},{5,4},{6,7},{7,6},{8,9},{9,8},{10,11... | collective-permute-start | bytes 196616 | tf_op jit(solution)/shard_map/ppermute | solution.py:500
  4.2 8.3 %collective-permute-start.1 = (f32[128,128]{1,0:T(8,128)S(1)}, f32[128,128]{1,0:T(8,128)S(1)}, u32[]{:S(2)}, u32[]{:S(2)}) collective-permute-start(f32[128,128]{1,0:T(8,128)S(1)} %get-tuple-element.39), channel_id=1, source_target_pairs={{1,2},{2,1},{3,4},{4,3},{5,6},{6,5},{7,8},{8,7},{9,10},{10,9},{11,... | collective-permute-start | bytes 196616 | tf_op jit(solution)/shard_map/ppermute | solution.py:500
  5.5 7.0 %collective-permute-start.2 = (f32[2,256]{1,0:T(2,128)S(1)}, f32[2,256]{1,0:T(2,128)S(1)}, u32[]{:S(2)}, u32[]{:S(2)}) collective-permute-start(f32[2,256]{1,0:T(2,128)S(1)} %get-tuple-element.40), channel_id=1, source_target_pairs={{0,112},{16,0},{32,16},{48,32},{64,48},{80,64},{96,80},{112,96},{1... | collective-permute-start | bytes 6152 | tf_op jit(solution)/shard_map/ppermute | solution.py:494
  13.1 22.2 %collective-permute-start.3 = (f32[72,256]{1,0:T(8,128)S(1)}, f32[72,256]{1,0:T(8,128)S(1)}, u32[]{:S(2)}, u32[]{:S(2)}) collective-permute-start(f32[72,256]{1,0:T(8,128)S(1)} %get-tuple-element.45), channel_id=1, source_target_pairs={{0,16},{16,0},{32,48},{48,32},{64,80},{80,64},{96,112},{112,96},{1... | collective-permute-start | bytes 221192 | tf_op jit(solution)/shard_map/ppermute | solution.py:500
  13.2 22.1 %collective-permute-start.4 = (f32[72,256]{1,0:T(8,128)S(1)}, f32[72,256]{1,0:T(8,128)S(1)}, u32[]{:S(2)}, u32[]{:S(2)}) collective-permute-start(f32[72,256]{1,0:T(8,128)S(1)} %get-tuple-element.46), channel_id=1, source_target_pairs={{16,32},{32,16},{48,64},{64,48},{80,96},{96,80},{112,0},{0,112},{1... | collective-permute-start | bytes 221192 | tf_op jit(solution)/shard_map/ppermute | solution.py:500
